TPU v7x, 128 devices: a whole 4x4x4 slice. The times are simulated.
128 devices in a mesh: ctx: 8 (over x, core), exp: 16 (over z, y).
Axes of the slice: x: 4, y: 4, z: 4, core: 2. Of those that a mesh axis runs over, the one named last changes fastest.
Arguments:
- hidden_in: bfloat16 [16, 1024, 2048], P('exp', 'ctx'), may hold values from -6 to 6
- grad_out: bfloat16 [16, 1024, 2048], P('exp', 'ctx'), may hold values from -6 to 6
- post_gain: float32 [2048], replicated, may hold values from 0.1 to 1.9
- route_ids: int32 [16, 1024, 10], P('exp', 'ctx'), may hold values from 0 to 511, as said below
- route_weight: float32 [16, 1024, 10], P('exp', 'ctx'), may hold values from 0.02 to 0.3
- gate_up: bfloat16 [128, 2048, 1024], P(('ctx', 'exp')), may hold values from -0.125 to 0.125
- down_proj: bfloat16 [128, 512, 2048], P(('ctx', 'exp')), may hold values from -0.25 to 0.25
- query_in: bfloat16 [16, 1024, 1024], P('exp', 'ctx'), may hold values from -6 to 6
- key_in: bfloat16 [16, 1024, 1024], P('exp', 'ctx'), may hold values from -6 to 6
- value_in: bfloat16 [16, 1024, 2048], P('exp', 'ctx'), may hold values from -6 to 6
- gate_in: bfloat16 [16, 1024, 2048], P('exp', 'ctx'), may hold values from -6 to 6
- decay_logit: bfloat16 [16, 1024, 16], P('exp', 'ctx'), may hold values from -12 to 0.5
- beta_logit: bfloat16 [16, 1024, 16], P('exp', 'ctx'), may hold values from -6 to 6
- head_gain: float32 [128], replicated, may hold values from 0.1 to 1.9
- out_proj: bfloat16 [2048, 2048], P(None, 'ctx'), may hold values from -0.125 to 0.125
Outputs:
- grad_hidden: bfloat16 [16, 1024, 2048], P('exp', 'ctx')
- grad_query: bfloat16 [16, 1024, 1024], P('exp', 'ctx')
- grad_key: bfloat16 [16, 1024, 1024], P('exp', 'ctx')
- grad_value: bfloat16 [16, 1024, 2048], P('exp', 'ctx')
- grad_gate: bfloat16 [16, 1024, 2048], P('exp', 'ctx')
- grad_decay: bfloat16 [16, 1024, 16], P('exp', 'ctx')
- grad_beta: bfloat16 [16, 1024, 16], P('exp', 'ctx')
- grad_gate_up: bfloat16 [128, 2048, 1024], P(('ctx', 'exp'))
- grad_down: bfloat16 [128, 512, 2048], P(('ctx', 'exp'))
- grad_out_proj: float32 [2048, 2048], P('exp', 'ctx')
Inputs may be any that keep to these rules, and one draw needn't show every extreme that they name: `route_ids`: each token names 10 different experts. The 128 positions of a sequence on one device name no expert more than 4 times, and one expert below 128, the same on every device, is named exactly 4 times by them.
All inputs are finite; a program needn't handle non-finite values.
Results may differ from a plain program's by a relative error of at most 0.014.
Values may be sent and summed in bfloat16 or wider, within the bound.
No kernel may reach another device: no remote copies, remote signals or barrier semaphores. Data moves between devices by JAX's collectives and lax.ppermute only.
A program may use at most 128 MiB of HBM per device.

v0:
```python
import jax
import jax.numpy as jnp
from jax import lax
from jax.sharding import PartitionSpec as P

BLOCK = 128


precise = lax.Precision.HIGHEST


def post_norm(hidden, gains):
    inverse_rms = lax.rsqrt(jnp.mean(hidden * hidden, axis=-1, keepdims=True) + 1e-06)
    return hidden * inverse_rms * gains


def block_step(memory, pieces):
    queries, key_rows, value_rows, strength, log_decay = pieces
    block_len = queries.shape[1]
    positions = jnp.arange(block_len)
    within = positions[:, None] >= positions[None, :]
    strict = positions[:, None] > positions[None, :]
    cumulative = jnp.cumsum(log_decay, axis=1)
    decay_mat = jnp.where(
        within,
        jnp.exp(jnp.where(within, cumulative[:, :, None] - cumulative[:, None, :], 0.0)),
        0.0,
    )
    inner_keys = jnp.einsum("htd,hsd->hts", key_rows, key_rows, precision=precise)
    lower_part = jnp.where(strict, strength[:, :, None] * decay_mat * inner_keys, 0.0)
    system = lower_part + jnp.eye(block_len, dtype=lower_part.dtype)
    recalled = jnp.einsum("hvd,htd->htv", memory, key_rows, precision=precise)
    rising = jnp.exp(cumulative)
    target = strength[:, :, None] * (value_rows - rising[:, :, None] * recalled)
    update = lax.linalg.triangular_solve(
        system, target, left_side=True, lower=True, unit_diagonal=True
    )
    scores = jnp.einsum("htd,hsd->hts", queries, key_rows, precision=precise) * decay_mat
    output = rising[:, :, None] * jnp.einsum("hvd,htd->htv", memory, queries, precision=precise)
    output = output + jnp.einsum("hts,hsv->htv", scores, update, precision=precise)
    last_log = cumulative[:, -1]
    fading = jnp.exp(last_log[:, None] - cumulative)
    memory = jnp.exp(last_log)[:, None, None] * memory + jnp.einsum(
        "hsv,hsd->hvd", update * fading[:, :, None], key_rows, precision=precise
    )
    return (memory, output)


def gated_delta(query_rows, key_rows, value_rows, gate_rows, decay_rows, beta_rows, head_gain):
    length = query_rows.shape[0]
    head_dim = head_gain.shape[0]
    key_heads = query_rows.shape[1] // head_dim
    value_heads = value_rows.shape[1] // head_dim
    group_size = value_heads // key_heads

    def unit_rows(tensor):
        shaped = tensor.reshape(length, key_heads, head_dim)
        shaped = shaped * lax.rsqrt(jnp.sum(shaped * shaped, axis=-1, keepdims=True) + 1e-06)
        return jnp.repeat(shaped, group_size, axis=1)

    queries_unit = unit_rows(query_rows) * head_dim ** (-0.5)
    keys_unit = unit_rows(key_rows)
    values_all = value_rows.reshape(length, value_heads, head_dim)
    strength = jax.nn.sigmoid(beta_rows)
    log_decay = -jax.nn.softplus(decay_rows)
    block_count = length // BLOCK

    def to_blocks(tensor):
        moved_axes = jnp.moveaxis(tensor, 0, 1)
        shaped = moved_axes.reshape((value_heads, block_count, BLOCK) + tensor.shape[2:])
        return jnp.moveaxis(shaped, 1, 0)

    initial = jnp.zeros((value_heads, head_dim, head_dim), query_rows.dtype)
    final_memory, outputs = lax.scan(
        block_step,
        initial,
        (
            to_blocks(queries_unit),
            to_blocks(keys_unit),
            to_blocks(values_all),
            to_blocks(strength),
            to_blocks(log_decay),
        ),
    )
    output = jnp.moveaxis(outputs, 0, 1).reshape(value_heads, length, head_dim)
    output = jnp.moveaxis(output, 0, 1)
    gates_all = gate_rows.reshape(length, value_heads, head_dim)
    normed = (
        output * lax.rsqrt(jnp.mean(output * output, axis=-1, keepdims=True) + 1e-06) * head_gain
    )
    return (normed * jax.nn.silu(gates_all)).reshape(length, value_heads * head_dim)


def expert_backward(rows_in, rows_grad, gate_up, down_proj):
    hidden_units = down_proj.shape[0]
    contract_rows = (((1,), (1,)), ((), ()))
    contract_cols = (((0,), (0,)), ((), ()))
    projected = jnp.dot(rows_in, gate_up, preferred_element_type=jnp.float32)
    gate_part = projected[:, :hidden_units]
    up_part = projected[:, hidden_units:]
    sigma = jax.nn.sigmoid(gate_part)
    activated = gate_part * sigma
    product = (activated * up_part).astype(jnp.bfloat16)
    grad_act = lax.dot_general(
        rows_grad, down_proj, contract_rows, preferred_element_type=jnp.float32
    )
    grad_gate_part = grad_act * up_part * sigma * (1.0 + gate_part * (1.0 - sigma))
    grad_up_part = grad_act * activated
    grad_projected = jnp.concatenate([grad_gate_part, grad_up_part], axis=1).astype(jnp.bfloat16)
    rows_back = lax.dot_general(
        grad_projected, gate_up, contract_rows, preferred_element_type=jnp.float32
    ).astype(jnp.bfloat16)
    weight_gate_up = lax.dot_general(
        rows_in, grad_projected, contract_cols, preferred_element_type=jnp.float32
    ).astype(jnp.bfloat16)
    weight_down = lax.dot_general(
        product, rows_grad, contract_cols, preferred_element_type=jnp.float32
    ).astype(jnp.bfloat16)
    return (rows_back, weight_gate_up, weight_down)


def body(
    hidden_in,
    grad_out,
    post_gain,
    route_ids,
    route_weight,
    gate_up,
    down_proj,
    query_in,
    key_in,
    value_in,
    gate_in,
    decay_logit,
    beta_logit,
    head_gain,
    out_proj,
):
    ctx_count = lax.axis_size("ctx")
    exp_count = lax.axis_size("exp")
    devices = ctx_count * exp_count
    tok_rows = hidden_in.shape[1]
    width = hidden_in.shape[2]
    top_count = route_ids.shape[2]
    capacity = max(3, tok_rows // 32)
    flat_hidden = hidden_in[0].astype(jnp.float32)
    normed, norm_back = jax.vjp(lambda tensor: post_norm(tensor, post_gain), flat_hidden)
    moe_input = normed.astype(jnp.bfloat16)
    slot_ids = route_ids[0].reshape(-1)
    slot_weights = route_weight[0].reshape(-1)
    slot_count = tok_rows * top_count
    owners = jnp.arange(devices, dtype=jnp.int32)
    matches = (slot_ids[:, None] == owners[None, :]).astype(jnp.int32)
    ranks = jnp.sum((jnp.cumsum(matches, axis=0) - 1) * matches, axis=1)
    sentinel = devices * capacity
    destination = jnp.where(slot_ids < devices, slot_ids * capacity + ranks, sentinel)
    source_slot = (
        jnp.full((sentinel,), slot_count, jnp.int32)
        .at[destination]
        .set(jnp.arange(slot_count, dtype=jnp.int32), mode="drop")
    )
    source_token = source_slot // top_count
    input_ext = jnp.concatenate([moe_input, jnp.zeros((1, width), jnp.bfloat16)], axis=0)
    grad_ext = jnp.concatenate([grad_out[0], jnp.zeros((1, width), jnp.bfloat16)], axis=0)
    weight_ext = jnp.concatenate([slot_weights, jnp.zeros((1,), jnp.float32)], axis=0)
    rows_in = input_ext[source_token]
    rows_grad = (
        grad_ext[source_token].astype(jnp.float32) * weight_ext[source_slot][:, None]
    ).astype(jnp.bfloat16)
    flat_shape = (devices, capacity, width)
    got_in, got_grad = (
        lax.all_to_all(
            rows_in.reshape(flat_shape), ("ctx", "exp"), split_axis=0, concat_axis=0, tiled=True
        ),
        lax.all_to_all(
            rows_grad.reshape(flat_shape), ("ctx", "exp"), split_axis=0, concat_axis=0, tiled=True
        ),
    )
    rows_back, grad_gate_up, grad_down = expert_backward(
        got_in.reshape(sentinel, width), got_grad.reshape(sentinel, width), gate_up[0], down_proj[0]
    )
    returned = lax.all_to_all(
        rows_back.reshape(flat_shape), ("ctx", "exp"), split_axis=0, concat_axis=0, tiled=True
    )
    returned_ext = jnp.concatenate(
        [returned.reshape(sentinel, width), jnp.zeros((1, width), jnp.bfloat16)], axis=0
    )
    slot_back = returned_ext[destination].astype(jnp.float32).reshape(tok_rows, top_count, width)
    moe_grad = jnp.sum(slot_back, axis=1)
    (norm_grad,) = norm_back(moe_grad)
    grad_hidden = (grad_out[0].astype(jnp.float32) + norm_grad).astype(jnp.bfloat16)[None]
    query_heads, key_heads, value_heads, gate_heads, decay_heads, beta_heads = (
        lax.all_to_all(query_in, "ctx", split_axis=2, concat_axis=1, tiled=True),
        lax.all_to_all(key_in, "ctx", split_axis=2, concat_axis=1, tiled=True),
        lax.all_to_all(value_in, "ctx", split_axis=2, concat_axis=1, tiled=True),
        lax.all_to_all(gate_in, "ctx", split_axis=2, concat_axis=1, tiled=True),
        lax.all_to_all(decay_logit, "ctx", split_axis=2, concat_axis=1, tiled=True),
        lax.all_to_all(beta_logit, "ctx", split_axis=2, concat_axis=1, tiled=True),
    )

    def forward(query_rows, key_rows, value_rows, gate_rows, decay_rows, beta_rows):
        return gated_delta(
            query_rows, key_rows, value_rows, gate_rows, decay_rows, beta_rows, head_gain
        )

    gated, core_back = jax.vjp(
        forward,
        query_heads[0].astype(jnp.float32),
        key_heads[0].astype(jnp.float32),
        value_heads[0].astype(jnp.float32),
        gate_heads[0].astype(jnp.float32),
        decay_heads[0].astype(jnp.float32),
        beta_heads[0].astype(jnp.float32),
    )
    hidden_all = lax.all_gather(grad_hidden, "ctx", axis=1, tiled=True)[0]
    grad_gated = jnp.dot(hidden_all, out_proj, preferred_element_type=jnp.float32)
    grad_q, grad_k, grad_v, grad_z, grad_d, grad_b = core_back(grad_gated)
    back_query, back_key, back_value, back_gate, back_decay, back_beta = (
        lax.all_to_all(
            grad_q.astype(jnp.bfloat16)[None], "ctx", split_axis=1, concat_axis=2, tiled=True
        ),
        lax.all_to_all(
            grad_k.astype(jnp.bfloat16)[None], "ctx", split_axis=1, concat_axis=2, tiled=True
        ),
        lax.all_to_all(
            grad_v.astype(jnp.bfloat16)[None], "ctx", split_axis=1, concat_axis=2, tiled=True
        ),
        lax.all_to_all(
            grad_z.astype(jnp.bfloat16)[None], "ctx", split_axis=1, concat_axis=2, tiled=True
        ),
        lax.all_to_all(
            grad_d.astype(jnp.bfloat16)[None], "ctx", split_axis=1, concat_axis=2, tiled=True
        ),
        lax.all_to_all(
            grad_b.astype(jnp.bfloat16)[None], "ctx", split_axis=1, concat_axis=2, tiled=True
        ),
    )
    gated_round = gated.astype(jnp.bfloat16)
    scale_factor = float(tok_rows * devices) ** (-0.5)
    grad_out_proj = lax.psum_scatter(
        (
            scale_factor
            * lax.dot_general(
                hidden_all,
                gated_round,
                (((0,), (0,)), ((), ())),
                preferred_element_type=jnp.float32,
            )
        ).astype(jnp.bfloat16),
        "exp",
        scatter_dimension=0,
        tiled=True,
    ).astype(jnp.float32)
    return (
        grad_hidden,
        back_query,
        back_key,
        back_value,
        back_gate,
        back_decay,
        back_beta,
        grad_gate_up[None],
        grad_down[None],
        grad_out_proj,
    )


def solution(mesh):
    placed = (
        P("exp", "ctx", None),
        P("exp", "ctx", None),
        P(),
        P("exp", "ctx", None),
        P("exp", "ctx", None),
        P(("ctx", "exp"), None, None),
        P(("ctx", "exp"), None, None),
        P("exp", "ctx", None),
        P("exp", "ctx", None),
        P("exp", "ctx", None),
        P("exp", "ctx", None),
        P("exp", "ctx", None),
        P("exp", "ctx", None),
        P(),
        P(None, "ctx"),
    )
    return jax.shard_map(
        body,
        mesh=mesh,
        in_specs=placed,
        out_specs=(
            P("exp", "ctx", None),
            P("exp", "ctx", None),
            P("exp", "ctx", None),
            P("exp", "ctx", None),
            P("exp", "ctx", None),
            P("exp", "ctx", None),
            P("exp", "ctx", None),
            P(("ctx", "exp"), None, None),
            P(("ctx", "exp"), None, None),
            P("exp", "ctx"),
        ),
        check_vma=False,
    )
```

profile of v0, /device:TPU:1, one launch (start us, length us, event | category | flops | bytes accessed | tf_op | source)
XLA Modules:
  0.0 1012.3 jit_solution(7308125901315340557)
XLA Ops:
  8.6 5.8 all-to-all-start.4
  40.6 11.0 %all-to-all-start.1 = ((bf16[128,4,2048]{2,1,0:T(4,128)(2,1)}), bf16[128,4,2048]{2,1,0:T(4,128)(2,1)}, u32[]{:S(2)}, u32[]{:S(2)}) async-start(bf16[128,4,2048]{2,1,0:T(4,128)(2,1)} %reshape.970), calls=%async_computation.1 | async-start | bytes 4194304 | tf_op jit(solution)/shard_map/all_to_all | solution.py:172
  67.5 13.0 %all-to-all-done.1 = bf16[128,4,2048]{2,1,0:T(4,128)(2,1)} async-done(((bf16[128,4,2048]{2,1,0:T(4,128)(2,1)}), bf16[128,4,2048]{2,1,0:T(4,128)(2,1)}, u32[]{:S(2)}, u32[]{:S(2)}) %all-to-all-start.1) | async-done | bytes 2097184 | tf_op jit(solution)/shard_map/all_to_all | solution.py:172
  80.5 6.4 all-to-all-start
  96.8 12.4 %reduce.29 = bf16[2048,128]{1,0:T(8,128)(2,1)} reduce(bf16[2048,1,128]{2,1,0:T(2,128)(2,1)S(1)} %bitcast.785, bf16[]{:T(256)} %broadcast.780), dimensions={1}, to_apply=%bitcast.544.reduce_sub_computation | reduce | bytes 1048578
  113.5 12.6 %reduce.30 = bf16[2048,128]{1,0:T(8,128)(2,1)} reduce(bf16[2048,1,128]{2,1,0:T(2,128)(2,1)S(1)} %bitcast.786, bf16[]{:T(256)} %broadcast.780), dimensions={1}, to_apply=%bitcast.546.reduce_sub_computation | reduce | bytes 1048578
  139.3 6.5 fusion.167
  165.9 6.1 fusion.169
  176.1 10.4 %all-to-all-start.2 = ((bf16[128,4,2048]{2,1,0:T(4,128)(2,1)}), bf16[128,4,2048]{2,1,0:T(4,128)(2,1)}, u32[]{:S(2)}, u32[]{:S(2)}) async-start(bf16[128,4,2048]{2,1,0:T(4,128)(2,1)} %reshape.972), calls=%async_computation.2 | async-start | bytes 4194304 | tf_op jit(solution)/shard_map/all_to_all | solution.py:182
  194.0 21.3 %all-to-all-done.2 = bf16[128,4,2048]{2,1,0:T(4,128)(2,1)} async-done(((bf16[128,4,2048]{2,1,0:T(4,128)(2,1)}), bf16[128,4,2048]{2,1,0:T(4,128)(2,1)}, u32[]{:S(2)}, u32[]{:S(2)}) %all-to-all-start.2) | async-done | bytes 2097184 | tf_op jit(solution)/shard_map/all_to_all | solution.py:182
  227.0 6.1 gather_fusion.3
  233.2 10.4 %reshape.986 = f32[128,10,2048]{2,1,0:T(8,128)} reshape(bf16[1280,2048]{1,0:T(8,128)(2,1)} %gather_fusion.3) | data formatting | bytes 15728640 | tf_op jit(solution)/shard_map/convert_element_type | solution.py:188
  243.6 9.9 reduce_sum.343
  271.7 256.6 %while.87 = (s32[]{:T(128)}, f32[2,128,128]{2,1,0:T(8,128)S(1)}, f32[8,2,128,128]{3,2,1,0:T(8,128)}, f32[8,2,128,128]{3,2,1,0:T(8,128)}, f32[8,2,128,128]{3,2,1,...) while((s32[]{:T(128)}, f32[2,128,128]{2,1,0:T(8,128)S(1)}, ...), condition=%wide.region_11.12_spmd.clone.clone, body=%wide.region_9.11_spmd.clone.clone.sunk | while | flops 353747584 | bytes 5875116 | solution.py:74
  276.8 19.7 %custom-call.32 = f32[2,1,128,128]{2,3,1,0:T(8,128)S(1)} custom-call(f32[2,1,128,128]{3,2,1,0:T(8,128)S(1)} %add_bitcast_fusion.2), custom_call_target="InvertDiagBlocksLowerTriangular" | custom-call | tf_op jit(solution)/shard_map/jvp()/while/body/eval_jaxpr/triangular_solve | solution.py:35
  308.9 19.7 %custom-call.32 = f32[2,1,128,128]{2,3,1,0:T(8,128)S(1)} custom-call(f32[2,1,128,128]{3,2,1,0:T(8,128)S(1)} %add_bitcast_fusion.2), custom_call_target="InvertDiagBlocksLowerTriangular" | custom-call | tf_op jit(solution)/shard_map/jvp()/while/body/eval_jaxpr/triangular_solve | solution.py:35
  341.0 19.7 %custom-call.32 = f32[2,1,128,128]{2,3,1,0:T(8,128)S(1)} custom-call(f32[2,1,128,128]{3,2,1,0:T(8,128)S(1)} %add_bitcast_fusion.2), custom_call_target="InvertDiagBlocksLowerTriangular" | custom-call | tf_op jit(solution)/shard_map/jvp()/while/body/eval_jaxpr/triangular_solve | solution.py:35
  373.0 19.7 %custom-call.32 = f32[2,1,128,128]{2,3,1,0:T(8,128)S(1)} custom-call(f32[2,1,128,128]{3,2,1,0:T(8,128)S(1)} %add_bitcast_fusion.2), custom_call_target="InvertDiagBlocksLowerTriangular" | custom-call | tf_op jit(solution)/shard_map/jvp()/while/body/eval_jaxpr/triangular_solve | solution.py:35
  405.0 19.7 %custom-call.32 = f32[2,1,128,128]{2,3,1,0:T(8,128)S(1)} custom-call(f32[2,1,128,128]{3,2,1,0:T(8,128)S(1)} %add_bitcast_fusion.2), custom_call_target="InvertDiagBlocksLowerTriangular" | custom-call | tf_op jit(solution)/shard_map/jvp()/while/body/eval_jaxpr/triangular_solve | solution.py:35
  437.1 19.7 %custom-call.32 = f32[2,1,128,128]{2,3,1,0:T(8,128)S(1)} custom-call(f32[2,1,128,128]{3,2,1,0:T(8,128)S(1)} %add_bitcast_fusion.2), custom_call_target="InvertDiagBlocksLowerTriangular" | custom-call | tf_op jit(solution)/shard_map/jvp()/while/body/eval_jaxpr/triangular_solve | solution.py:35
  469.1 19.7 %custom-call.32 = f32[2,1,128,128]{2,3,1,0:T(8,128)S(1)} custom-call(f32[2,1,128,128]{3,2,1,0:T(8,128)S(1)} %add_bitcast_fusion.2), custom_call_target="InvertDiagBlocksLowerTriangular" | custom-call | tf_op jit(solution)/shard_map/jvp()/while/body/eval_jaxpr/triangular_solve | solution.py:35
  501.2 19.7 %custom-call.32 = f32[2,1,128,128]{2,3,1,0:T(8,128)S(1)} custom-call(f32[2,1,128,128]{3,2,1,0:T(8,128)S(1)} %add_bitcast_fusion.2), custom_call_target="InvertDiagBlocksLowerTriangular" | custom-call | tf_op jit(solution)/shard_map/jvp()/while/body/eval_jaxpr/triangular_solve | solution.py:35
  553.3 358.4 %while.88 = (s32[]{:T(128)}, f32[2,128,128]{2,1,0:T(8,128)S(1)}, f32[8,2,128,128]{3,2,1,0:T(8,128)}, f32[8,2,128,128]{3,2,1,0:T(8,128)}, bf16[8,2,128,128]{3,2,0...) while((s32[]{:T(128)}, f32[2,128,128]{2,1,0:T(8,128)S(1)}, ...), condition=%wide.region_25.27_spmd.clone.clone, body=%wide.region_14.26_spmd.clone.clone.sunk | while | flops 756860032 | bytes 11536937 | solution.py:74
  563.1 19.7 %custom-call.33 = f32[2,1,128,128]{2,3,1,0:T(8,128)S(1)} custom-call(f32[2,1,128,128]{3,2,1,0:T(8,128)S(1)} %fusion.321), custom_call_target="InvertDiagBlocksLowerTriangular" | custom-call | tf_op jit(solution)/shard_map/transpose(jvp())/while/body/eval_jaxpr/triangular_solve/custom-call.0 | solution.py:35
  607.8 19.7 %custom-call.33 = f32[2,1,128,128]{2,3,1,0:T(8,128)S(1)} custom-call(f32[2,1,128,128]{3,2,1,0:T(8,128)S(1)} %fusion.321), custom_call_target="InvertDiagBlocksLowerTriangular" | custom-call | tf_op jit(solution)/shard_map/transpose(jvp())/while/body/eval_jaxpr/triangular_solve/custom-call.0 | solution.py:35
  652.6 19.7 %custom-call.33 = f32[2,1,128,128]{2,3,1,0:T(8,128)S(1)} custom-call(f32[2,1,128,128]{3,2,1,0:T(8,128)S(1)} %fusion.321), custom_call_target="InvertDiagBlocksLowerTriangular" | custom-call | tf_op jit(solution)/shard_map/transpose(jvp())/while/body/eval_jaxpr/triangular_solve/custom-call.0 | solution.py:35
  697.4 19.7 %custom-call.33 = f32[2,1,128,128]{2,3,1,0:T(8,128)S(1)} custom-call(f32[2,1,128,128]{3,2,1,0:T(8,128)S(1)} %fusion.321), custom_call_target="InvertDiagBlocksLowerTriangular" | custom-call | tf_op jit(solution)/shard_map/transpose(jvp())/while/body/eval_jaxpr/triangular_solve/custom-call.0 | solution.py:35
  742.2 19.7 %custom-call.33 = f32[2,1,128,128]{2,3,1,0:T(8,128)S(1)} custom-call(f32[2,1,128,128]{3,2,1,0:T(8,128)S(1)} %fusion.321), custom_call_target="InvertDiagBlocksLowerTriangular" | custom-call | tf_op jit(solution)/shard_map/transpose(jvp())/while/body/eval_jaxpr/triangular_solve/custom-call.0 | solution.py:35
  786.9 19.7 %custom-call.33 = f32[2,1,128,128]{2,3,1,0:T(8,128)S(1)} custom-call(f32[2,1,128,128]{3,2,1,0:T(8,128)S(1)} %fusion.321), custom_call_target="InvertDiagBlocksLowerTriangular" | custom-call | tf_op jit(solution)/shard_map/transpose(jvp())/while/body/eval_jaxpr/triangular_solve/custom-call.0 | solution.py:35
  831.7 19.7 %custom-call.33 = f32[2,1,128,128]{2,3,1,0:T(8,128)S(1)} custom-call(f32[2,1,128,128]{3,2,1,0:T(8,128)S(1)} %fusion.321), custom_call_target="InvertDiagBlocksLowerTriangular" | custom-call | tf_op jit(solution)/shard_map/transpose(jvp())/while/body/eval_jaxpr/triangular_solve/custom-call.0 | solution.py:35
  876.6 19.7 %custom-call.33 = f32[2,1,128,128]{2,3,1,0:T(8,128)S(1)} custom-call(f32[2,1,128,128]{3,2,1,0:T(8,128)S(1)} %fusion.321), custom_call_target="InvertDiagBlocksLowerTriangular" | custom-call | tf_op jit(solution)/shard_map/transpose(jvp())/while/body/eval_jaxpr/triangular_solve/custom-call.0 | solution.py:35
  984.4 6.0 convert_bitcast_fusion.1
  (767 shorter events, 542.3 us)
Async XLA Ops:
  7.2 147.5 %copy-start = (bf16[1,512,2048]{2,1,0:T(8,128)(2,1)S(1)}, bf16[1,512,2048]{2,1,0:T(8,128)(2,1)}, u32[]{:S(2)}) copy-start(bf16[1,512,2048]{2,1,0:T(8,128)(2,1)} %param.27) | copy-start | bytes 6291460
  8.6 19.7 %all-to-all-start.4 = ((bf16[8,2,128]{2,1,0:T(2,128)(2,1)}), bf16[8,2,128]{2,1,0:T(2,128)(2,1)S(1)}, u32[]{:S(2)}, u32[]{:S(2)}) async-start(bf16[8,2,128]{2,1,0:T(2,128)(2,1)} %bitcast.618), calls=%async_computation.4 | async-start | bytes 8192 | tf_op jit(solution)/shard_map/all_to_all | solution.py:198
  21.5 6.2 copy-start.25
  28.4 12.3 %all-to-all-start.3 = ((bf16[8,2,128]{2,1,0:T(2,128)(2,1)}), bf16[8,2,128]{2,1,0:T(2,128)(2,1)S(1)}, u32[]{:S(2)}, u32[]{:S(2)}) async-start(bf16[8,2,128]{2,1,0:T(2,128)(2,1)} %bitcast.619), calls=%async_computation.3 | async-start | bytes 8192 | tf_op jit(solution)/shard_map/all_to_all | solution.py:197
  40.6 11.0 %copy-start.14 = (bf16[1,128,2048]{2,1,0:T(8,128)(2,1)S(1)}, bf16[1,128,2048]{2,1,0:T(8,128)(2,1)}, u32[]{:S(2)}) copy-start(bf16[1,128,2048]{2,1,0:T(8,128)(2,1)} %param.22) | copy-start | bytes 1572868
  40.6 39.9 %all-to-all-start.1 = ((bf16[128,4,2048]{2,1,0:T(4,128)(2,1)}), bf16[128,4,2048]{2,1,0:T(4,128)(2,1)}, u32[]{:S(2)}, u32[]{:S(2)}) async-start(bf16[128,4,2048]{2,1,0:T(4,128)(2,1)} %reshape.970), calls=%async_computation.1 | async-start | bytes 4194304 | tf_op jit(solution)/shard_map/all_to_all | solution.py:172
  67.5 19.4 %copy-start.21 = (bf16[1,128,1024]{2,1,0:T(8,128)(2,1)S(1)}, bf16[1,128,1024]{2,1,0:T(8,128)(2,1)}, u32[]{:S(2)}) copy-start(bf16[1,128,1024]{2,1,0:T(8,128)(2,1)} %param.28) | copy-start | bytes 786436
  80.5 54.0 %all-to-all-start = ((bf16[128,4,2048]{2,1,0:T(4,128)(2,1)}), bf16[128,4,2048]{2,1,0:T(4,128)(2,1)}, u32[]{:S(2)}, u32[]{:S(2)}) async-start(bf16[128,4,2048]{2,1,0:T(4,128)(2,1)} %multiply_convert_fusion), calls=%async_computation | async-start | bytes 4194304 | tf_op jit(solution)/shard_map/all_to_all | solution.py:175
  134.5 15.4 %all-to-all-start.7 = ((bf16[8,2,8192]{2,1,0:T(2,128)(2,1)}), bf16[8,2,8192]{2,1,0:T(2,128)(2,1)S(1)}, u32[]{:S(2)}, u32[]{:S(2)}) async-start(bf16[8,2,8192]{2,1,0:T(2,128)(2,1)} %reshape.1066), calls=%async_computation.7 | async-start | bytes 524288 | tf_op jit(solution)/shard_map/all_to_all | solution.py:193
  149.9 11.3 %all-to-all-start.5 = ((bf16[8,2,8192]{2,1,0:T(2,128)(2,1)}), bf16[8,2,8192]{2,1,0:T(2,128)(2,1)S(1)}, u32[]{:S(2)}, u32[]{:S(2)}) async-start(bf16[8,2,8192]{2,1,0:T(2,128)(2,1)} %reshape.1072), calls=%async_computation.5 | async-start | bytes 524288 | tf_op jit(solution)/shard_map/all_to_all | solution.py:194
  159.2 12.8 %copy-start.31 = (bf16[512,512]{0,1:T(8,128)(2,1)}, bf16[512,512]{0,1:T(8,128)(2,1)S(1)}, u32[]{:S(2)}) copy-start(bf16[512,512]{0,1:T(8,128)(2,1)S(1)} %get-tuple-element.2414) | copy-start | bytes 1572868
  161.2 10.8 %copy-start.18 = (bf16[8,2,8192]{2,1,0:T(2,128)(2,1)}, bf16[8,2,8192]{2,1,0:T(2,128)(2,1)S(1)}, u32[]{:S(2)}) copy-start(bf16[8,2,8192]{2,1,0:T(2,128)(2,1)S(1)} %all-to-all-done.5) | copy-start | bytes 786436
  161.2 14.9 %all-to-all-start.6 = ((bf16[8,2,16384]{2,1,0:T(2,128)(2,1)}), bf16[8,2,16384]{2,1,0:T(2,128)(2,1)S(1)}, u32[]{:S(2)}, u32[]{:S(2)}) async-start(bf16[8,2,16384]{2,1,0:T(2,128)(2,1)} %reshape.1074), calls=%async_computation.6 | async-start | bytes 1048576 | tf_op jit(solution)/shard_map/all_to_all | solution.py:195
  176.1 39.3 %all-to-all-start.2 = ((bf16[128,4,2048]{2,1,0:T(4,128)(2,1)}), bf16[128,4,2048]{2,1,0:T(4,128)(2,1)}, u32[]{:S(2)}, u32[]{:S(2)}) async-start(bf16[128,4,2048]{2,1,0:T(4,128)(2,1)} %reshape.972), calls=%async_computation.2 | async-start | bytes 4194304 | tf_op jit(solution)/shard_map/all_to_all | solution.py:182
  215.3 312.9 %all-to-all-start.8 = ((bf16[8,2,16384]{2,1,0:T(2,128)(2,1)}), bf16[8,2,16384]{2,1,0:T(2,128)(2,1)}, u32[]{:S(2)}, u32[]{:S(2)}) async-start(bf16[8,2,16384]{2,1,0:T(2,128)(2,1)} %reshape.1076), calls=%async_computation.8 | async-start | bytes 1048576 | tf_op jit(solution)/shard_map/all_to_all | solution.py:196
  220.9 319.9 %all-gather.2.cloned.1.call-start = ((), (), s32[]{:S(2)}) async-start(), calls=%async_computation.16 | async-start | bytes 4718592 | tf_op jit(solution)/shard_map/all_gather | solution.py:215
  243.5 9.9 copy-start.6
  243.5 10.1 copy-start.29
  243.5 10.1 %copy-start.15 = (bf16[1,128,2048]{2,1,0:T(8,128)(2,1)S(1)}, bf16[1,128,2048]{2,1,0:T(8,128)(2,1)}, u32[]{:S(2)}) copy-start(bf16[1,128,2048]{2,1,0:T(8,128)(2,1)} %param.22) | copy-start | bytes 1572868
  243.6 10.1 %copy-start.27 = (f32[128]{0:T(128)S(1)}, f32[128]{0:T(128)}, u32[]{:S(2)}) copy-start(f32[128]{0:T(128)} %copy-done.26) | copy-start | bytes 1540
  528.3 7.4 copy-start.4
  911.7 11.7 %copy-start.20 = (bf16[1024,2,128]{0,2,1:T(8,128)(2,1)S(1)}, bf16[1024,2,128]{0,2,1:T(8,128)(2,1)}, u32[]{:S(2)}) copy-start(bf16[1024,2,128]{0,2,1:T(8,128)(2,1)} %get-tuple-element.2416) | copy-start | bytes 1572868
  918.1 15.2 %all-to-all-start.13 = ((bf16[8,2,128]{2,1,0:T(2,128)(2,1)}), bf16[8,2,128]{2,1,0:T(2,128)(2,1)S(1)}, u32[]{:S(2)}, u32[]{:S(2)}) async-start(bf16[8,2,128]{2,1,0:T(2,128)(2,1)} %reshape.1086), calls=%async_computation.13 | async-start | bytes 8192 | tf_op jit(solution)/shard_map/all_to_all | solution.py:231
  923.0 80.7 %reduce-scatter.2.cloned.1.call-start = ((), (), s32[]{:S(2)}) async-start(), calls=%async_computation.17 | async-start | bytes 1114112 | tf_op jit(solution)/shard_map/reduce_scatter | solution.py:240
  933.3 9.3 all-to-all-start.14
  942.6 10.5 %all-to-all-start.9 = ((bf16[8,2,8192]{2,1,0:T(2,128)(2,1)}), bf16[8,2,8192]{2,1,0:T(2,128)(2,1)S(1)}, u32[]{:S(2)}, u32[]{:S(2)}) async-start(bf16[8,2,8192]{2,1,0:T(2,128)(2,1)} %reshape.1078), calls=%async_computation.9 | async-start | bytes 524288 | tf_op jit(solution)/shard_map/all_to_all | solution.py:219
  946.6 11.1 %copy-start.16 = (bf16[8,2,128,128]{3,2,0,1:T(8,128)(2,1)S(1)}, bf16[8,2,128,128]{3,2,0,1:T(8,128)(2,1)}, u32[]{:S(2)}) copy-start(bf16[8,2,128,128]{3,2,0,1:T(8,128)(2,1)} %get-tuple-element.1274) | copy-start | bytes 1572868
  953.2 11.0 %all-to-all-start.10 = ((bf16[8,2,8192]{2,1,0:T(2,128)(2,1)}), bf16[8,2,8192]{2,1,0:T(2,128)(2,1)S(1)}, u32[]{:S(2)}, u32[]{:S(2)}) async-start(bf16[8,2,8192]{2,1,0:T(2,128)(2,1)} %reshape.1080), calls=%async_computation.10 | async-start | bytes 524288 | tf_op jit(solution)/shard_map/all_to_all | solution.py:222
  964.2 15.1 %all-to-all-start.11 = ((bf16[8,2,16384]{2,1,0:T(2,128)(2,1)}), bf16[8,2,16384]{2,1,0:T(2,128)(2,1)S(1)}, u32[]{:S(2)}, u32[]{:S(2)}) async-start(bf16[8,2,16384]{2,1,0:T(2,128)(2,1)} %reshape.1082), calls=%async_computation.11 | async-start | bytes 1048576 | tf_op jit(solution)/shard_map/all_to_all | solution.py:225
  974.4 10.0 copy-start.32
  979.3 18.8 %all-to-all-start.12 = ((bf16[8,2,16384]{2,1,0:T(2,128)(2,1)}), bf16[8,2,16384]{2,1,0:T(2,128)(2,1)}, u32[]{:S(2)}, u32[]{:S(2)}) async-start(bf16[8,2,16384]{2,1,0:T(2,128)(2,1)} %reshape.1084), calls=%async_computation.12 | async-start | bytes 1048576 | tf_op jit(solution)/shard_map/all_to_all | solution.py:228
  998.2 7.1 copy-start.1
  (19 other events, 61.6 us)
Sparse Core Ops, SparseCore 0:
  255.0 29.9 all-gather.1
  928.2 68.9 reduce-scatter.1
where the time goes:
time: 1020 us; the launch traced here: 1010 us
  other arithmetic  446 us (44%)
  matrix products  234 us (23%)
  local copies, waits for them, and re-layouts  188 us (18%)
  starting transfers between devices  86.3 us (8%)
  waiting for transfers between devices  40.7 us (4%)
  between operations  15.4 us (2%)
    another operation x64, other arithmetic, block_step(): lax.linalg.triangular_solve(system, target, left_side=True, lower=True, u...  325 us
    unnamed x13, other arithmetic  46.4 us
    unnamed x113, local copies, waits for them, and re-layouts  37.4 us
    dot_general x24, matrix products, block_step(): jnp.einsum('htd,hsd->hts', queries, key_rows, precision=precise) * decay_mat  35.6 us
    dot_general x24, matrix products, block_step(): jnp.einsum('hts,hsv->htv', scores, update, precision=precise)  30.9 us
    dot_general x24, matrix products, block_step(): recalled = jnp.einsum('hvd,htd->htv', memory, key_rows, precision=precise)  30.3 us
    dot_general x24, matrix products, block_step(): jnp.einsum('hvd,htd->htv', memory, queries, precision=precise)  29 us
    dot_general x24, matrix products, block_step(): jnp.einsum('htd,hsd->hts', key_rows, key_rows, precision=precise)  28.2 us
  transfers between devices with their start and end apart: 17, of which 6 were waited for; matrix products, arithmetic and copies ran while one was open for 48% of the time, Pallas kernels for 0%

commit v1 on v0

v1 whole, which is shorter than its diff:
```python
import functools

import jax
import jax.numpy as jnp
from jax import lax
from jax.experimental import pallas as pl
from jax.experimental.pallas import tpu as pltpu
from jax.sharding import PartitionSpec as P

F32 = jnp.float32
BF16 = jnp.bfloat16
EPS = 1e-6
MIB = 1 << 20

NN = (((1,), (0,)), ((), ()))
NT = (((1,), (1,)), ((), ()))
TN = (((0,), (0,)), ((), ()))


def dot(a, b, dims=NN):
    return lax.dot_general(a, b, dims, preferred_element_type=F32)


def halves(x):
    high = x.astype(BF16)
    return high, (x - high.astype(F32)).astype(BF16)


def dot_exact_left(a, b):
    high, low = halves(b)
    return dot(jnp.concatenate([a, a], axis=1), jnp.concatenate([high, low], axis=0))


def dot_split(a, b):
    ah, al = halves(a)
    bh, bl = halves(b)
    return dot(jnp.concatenate([ah, al, ah], axis=1), jnp.concatenate([bh, bh, bl], axis=0))


def dot_ones(a, ones):
    high = a.astype(BF16)
    rest = a - high.astype(F32)
    middle = rest.astype(BF16)
    low = (rest - middle.astype(F32)).astype(BF16)
    return dot(
        jnp.concatenate([high, middle, low], axis=1), jnp.concatenate([ones] * 3, axis=0)
    )


def iota(shape, axis):
    return lax.broadcasted_iota(jnp.int32, shape, axis)


def mask01(cond):
    return jnp.where(cond, 1.0, 0.0).astype(BF16)


def params(limit_mib=56, **kwargs):
    return pltpu.CompilerParams(vmem_limit_bytes=limit_mib * MIB, **kwargs)


def pack_kernel(q_ref, k_ref, v_ref, z_ref, decay_ref, beta_ref, out_ref):
    groups = out_ref.shape[0]
    heads = decay_ref.shape[1]
    row = iota((8 * groups, heads), 0)
    head = iota((8 * groups, heads), 1)
    kind = row % 8
    own = 2 * (row // 8) + kind % 2
    is_beta = (kind == 2) | (kind == 3)
    pick_decay = mask01((head == own) & ~is_beta)
    pick_beta = mask01((head == own) & is_beta)
    rows = dot(pick_decay, decay_ref[...], NT) + dot(pick_beta, beta_ref[...], NT)
    rows = rows.astype(BF16)
    for i in range(groups):
        out_ref[i, 0:128, 0:128] = q_ref[:, 128 * i : 128 * (i + 1)]
        out_ref[i, 0:128, 128:256] = k_ref[:, 128 * i : 128 * (i + 1)]
        out_ref[i, 0:128, 256:512] = v_ref[:, 256 * i : 256 * (i + 1)]
        out_ref[i, 0:128, 512:768] = z_ref[:, 256 * i : 256 * (i + 1)]
        out_ref[i, 128:136, 0:128] = rows[8 * i : 8 * (i + 1), :]
        out_ref[i, 128:136, 128:768] = jnp.zeros((8, 640), BF16)


def unpack_kernel(in_ref, q_ref, k_ref, v_ref, z_ref, decay_ref, beta_ref):
    groups = in_ref.shape[0]
    heads = decay_ref.shape[1]
    rows = []
    for i in range(groups):
        q_ref[:, 128 * i : 128 * (i + 1)] = in_ref[i, 0:128, 0:128]
        k_ref[:, 128 * i : 128 * (i + 1)] = in_ref[i, 0:128, 128:256]
        v_ref[:, 256 * i : 256 * (i + 1)] = in_ref[i, 0:128, 256:512]
        z_ref[:, 256 * i : 256 * (i + 1)] = in_ref[i, 0:128, 512:768]
        rows.append(in_ref[i, 128:136, 0:128].astype(F32))
    rows = jnp.concatenate(rows, axis=0).astype(BF16)
    row = iota((8 * groups, heads), 0)
    head = iota((8 * groups, heads), 1)
    kind = row % 8
    own = 2 * (row // 8) + kind % 2
    decay_ref[...] = dot(rows, mask01((head == own) & (kind < 2)), TN).astype(BF16)
    beta_ref[...] = dot(rows, mask01((head == own) & ((kind == 2) | (kind == 3))), TN).astype(BF16)


def slot_code(ids_ref, weight_ref):
    tokens, top = ids_ref.shape
    held = 128
    expert = iota((tokens, held), 1)
    named = jnp.zeros((tokens, held), F32)
    weight = jnp.zeros((tokens, held), F32)
    for k in range(top):
        hit = ids_ref[:, k : k + 1] == expert
        named = jnp.where(hit, 1.0, named)
        if weight_ref is not None:
            weight = jnp.where(hit, weight_ref[:, k : k + 1], weight)
    earlier = mask01(iota((tokens, tokens), 0) > iota((tokens, tokens), 1))
    rank = dot(earlier, named.astype(BF16))
    return jnp.where(named > 0.5, rank, -1.0), weight


def dispatch_kernel(hidden_ref, grad_ref, gain_ref, ids_ref, weight_ref, out_ref, both, pick, scale):
    rows = out_ref.shape[0]
    tokens, width = hidden_ref.shape
    cols = out_ref.shape[1]
    step = pl.program_id(0)

    @pl.when(step == 0)
    def _():
        hidden = hidden_ref[...].astype(F32)
        inverse = lax.rsqrt(jnp.mean(hidden * hidden, axis=-1, keepdims=True) + EPS)
        both[0:tokens, :] = (hidden * inverse * gain_ref[...]).astype(BF16)
        both[tokens:, :] = grad_ref[...]
        code, weight = slot_code(ids_ref, weight_ref)
        held = code.shape[1]
        spread = mask01(iota((rows, held), 0) // 8 == iota((rows, held), 1))
        wide = dot(spread, code.astype(BF16), NT)
        row = iota((rows, tokens), 0) % 8
        hit = wide == (row % 4).astype(F32)
        high = weight.astype(BF16)
        rest = weight - high.astype(F32)
        middle = rest.astype(BF16)
        low = (rest - middle.astype(F32)).astype(BF16)
        wide_weight = dot(spread, high, NT) + dot(spread, middle, NT) + dot(spread, low, NT)
        is_grad = row >= 4
        pick[:, 0:tokens] = mask01(hit & ~is_grad)
        pick[:, tokens:] = mask01(hit & is_grad)
        total = jnp.sum(jnp.where(hit, wide_weight, 0.0), axis=-1, keepdims=True)
        scale[...] = jnp.where(iota((rows, 1), 0) % 8 >= 4, total, 1.0)

    start = pl.multiple_of(step * cols, cols)
    chunk = dot(pick[...], both[:, pl.ds(start, cols)])
    out_ref[...] = (chunk * scale[...]).astype(BF16)


def expert_kernel(
    got_ref, up_hbm, down_hbm, back_ref, rows_ref, grads_ref, act_ref, gproj_ref,
    up_ref, down_ref, sems,
):
    hidden_units = down_ref.shape[0]
    width = down_ref.shape[1]
    copy_up = pltpu.make_async_copy(up_hbm, up_ref, sems.at[0])
    copy_down = pltpu.make_async_copy(down_hbm, down_ref, sems.at[1])
    copy_up.start()
    copy_down.start()
    count = rows_ref.shape[0]
    chunks = count // 64
    r = iota((128, 128), 0)
    c = iota((128, 128), 1)
    source = ((r % 64) // 4) * 8 + (r // 64) * 4 + r % 4
    gather = mask01(c == source)
    scatter = mask01(r == ((c % 64) // 4) * 8 + (c // 64) * 4 + c % 4)

    def separate(i, carry):
        block = got_ref[pl.ds(pl.multiple_of(i * 128, 128), 128), :]
        moved = dot(gather, block).astype(BF16)
        at = pl.multiple_of(i * 64, 64)
        rows_ref[pl.ds(at, 64), :] = moved[0:64]
        grads_ref[pl.ds(at, 64), :] = moved[64:128]
        return carry

    lax.fori_loop(0, chunks, separate, 0)
    copy_up.wait()
    copy_down.wait()

    def middle(j, carry):
        at = pl.multiple_of(j * 256, 256)
        gate = dot(rows_ref[...], up_ref[:, pl.ds(at, 256)])
        up = dot(rows_ref[...], up_ref[:, pl.ds(hidden_units + at, 256)])
        grad_act = dot(grads_ref[...], down_ref[pl.ds(at, 256), :], NT)
        sigma = jax.nn.sigmoid(gate)
        activated = gate * sigma
        act_ref[:, pl.ds(at, 256)] = (activated * up).astype(BF16)
        gproj_ref[:, pl.ds(at, 256)] = (
            grad_act * up * sigma * (1.0 + gate * (1.0 - sigma))
        ).astype(BF16)
        gproj_ref[:, pl.ds(hidden_units + at, 256)] = (grad_act * activated).astype(BF16)
        return carry

    lax.fori_loop(0, hidden_units // 256, middle, 0)

    def backward(j, carry):
        at = pl.multiple_of(j * 256, 256)
        left = dot(gproj_ref[...], up_ref[pl.ds(at, 256), :], NT).astype(BF16)
        right = dot(gproj_ref[...], up_ref[pl.ds(width // 2 + at, 256), :], NT).astype(BF16)
        for i in range(chunks):
            block = jnp.concatenate(
                [left[64 * i : 64 * (i + 1)], right[64 * i : 64 * (i + 1)]], axis=0
            )
            back_ref[128 * i : 128 * (i + 1), pl.ds(at, 256)] = dot(scatter, block).astype(BF16)
        return carry

    lax.fori_loop(0, width // 512, backward, 0)


def combine_kernel(
    back_ref, hidden_ref, grad_ref, gain_ref, ids_ref, proj_ref, hidden_grad_ref, out_ref
):
    tokens, width = hidden_ref.shape

    @pl.when(pl.program_id(0) == 0)
    def _():
        code, _ = slot_code(ids_ref, None)
        held = code.shape[1]
        rows = 8 * held
        spread = mask01(iota((held, rows), 0) == iota((held, rows), 1) // 8)
        wide = dot(code.astype(BF16), spread)
        place = iota((tokens, rows), 1) % 8
        hit = wide == (place % 4).astype(F32)
        first = mask01(hit & (place < 4))
        second = mask01(hit & (place >= 4))
        gain = gain_ref[...]
        hidden = hidden_ref[...].astype(F32)
        inverse = lax.rsqrt(jnp.mean(hidden * hidden, axis=-1, keepdims=True) + EPS)
        moe_grad = jnp.concatenate([dot(first, back_ref[...]), dot(second, back_ref[...])], axis=1)
        scaled = moe_grad * gain
        inner = jnp.mean(scaled * hidden, axis=-1, keepdims=True)
        norm_grad = inverse * scaled - hidden * (inverse * inverse * inverse * inner)
        hidden_grad_ref[...] = (grad_ref[...].astype(F32) + norm_grad).astype(BF16)

    out_ref[0] = dot(hidden_grad_ref[...], proj_ref[0]).astype(BF16)


def triangle(shape, strict=False):
    if strict:
        return iota(shape, 0) > iota(shape, 1)
    return iota(shape, 0) >= iota(shape, 1)


def vectors(att_ref, rows_scr, cols_scr):
    blocks = att_ref.shape[0]
    logits = jnp.concatenate(
        [att_ref[n, 128:136, 0:128].astype(F32) for n in range(blocks)], axis=0
    )
    kind = iota(logits.shape, 0) % 8
    upto = mask01(iota((128, 128), 0) <= iota((128, 128), 1))
    softplus = jnp.maximum(logits, 0.0) + jnp.log1p(jnp.exp(-jnp.abs(logits)))
    cumulative = dot_ones(-softplus, upto)
    strength = jax.nn.sigmoid(logits)
    fading = jnp.exp(cumulative[:, 127:128] - cumulative)
    rows = jnp.where(
        kind < 2,
        cumulative,
        jnp.where(kind < 4, strength, jnp.where(kind < 6, jnp.exp(cumulative), fading)),
    )
    cols = jnp.transpose(
        jnp.concatenate([rows, jnp.zeros((128 - rows.shape[0], 128), F32)], axis=0)
    )
    for n in range(blocks):
        rows_scr[n] = rows[8 * n : 8 * (n + 1)]
        cols_scr[n, :, 0:8] = cols[:, 8 * n : 8 * (n + 1)]
    return logits


def unit_scale(x, factor):
    xf = x.astype(F32)
    return lax.rsqrt(jnp.sum(xf * xf, axis=-1, keepdims=True) + EPS) * factor


def decay_matrix(col, row):
    within = triangle((128, 128))
    return jnp.where(within, jnp.exp(jnp.minimum(col - row, 0.0)), 0.0)


def forward_kernel(
    att_ref, gain_ref,
    gated_ref, tinv_ref, pair_ref, upd_ref, eks_ref, eqs_ref, mem_ref, core_ref,
    rows_scr, cols_scr, tri_scr, score_scr, state_scr,
):
    blocks = att_ref.shape[0]
    dim = 128
    vectors(att_ref, rows_scr, cols_scr)
    strict = triangle((dim, dim), strict=True)
    r = iota((dim, dim), 0)
    c = iota((dim, dim), 1)

    def inverse(n, carry):
        q = att_ref[n, 0:128, 0:128]
        k = att_ref[n, 0:128, 128:256]
        rows = rows_scr[n]
        cols = cols_scr[n]
        rk = unit_scale(k, 1.0)
        rq = unit_scale(q, dim**-0.5)
        rk_row = jnp.transpose(jnp.broadcast_to(rk, (dim, dim)))
        both = dot(jnp.concatenate([k, q], axis=0), k, NT)
        kk = both[0:128] * (rk * rk_row)
        qk = both[128:256] * (rq * rk_row)
        for h in range(2):
            decay = decay_matrix(cols[:, h : h + 1], rows[h : h + 1, :])
            low = jnp.where(strict, cols[:, 2 + h : 3 + h] * decay * kk, 0.0)
            inv = jnp.where(r == c, 1.0, 0.0) - jnp.where(r // 2 == c // 2, low, 0.0)
            size = 2
            while size < dim:
                level = (r // (2 * size) == c // (2 * size)) & (r // size != c // size)
                inv = inv - dot_split(dot_split(inv, jnp.where(level, low, 0.0)), inv)
                size *= 2
            tri_scr[n, :, 128 * h : 128 * (h + 1)] = inv
            score_scr[n, :, 128 * h : 128 * (h + 1)] = qk * decay
        return carry

    lax.fori_loop(0, blocks, inverse, 0)
    state_scr[...] = jnp.zeros_like(state_scr)
    gain = gain_ref[...]

    def advance(n, carry):
        q = att_ref[n, 0:128, 0:128]
        k = att_ref[n, 0:128, 128:256]
        cols = cols_scr[n]
        rows = rows_scr[n]
        rk = unit_scale(k, 1.0)
        rq = unit_scale(q, dim**-0.5)
        state = state_scr[...]
        mem_ref[n] = state.astype(BF16)
        recalled = dot_exact_left(jnp.concatenate([k, q], axis=0), state)
        kt = jnp.transpose(k)
        writes = []
        for h in range(2):
            at = slice(128 * h, 128 * (h + 1))
            beta = cols[:, 2 + h : 3 + h]
            rising = cols[:, 4 + h : 5 + h]
            fading = cols[:, 6 + h : 7 + h]
            eks = recalled[0:128, at] * (rk * rising)
            eqs = recalled[128:256, at] * (rq * rising)
            target = att_ref[n, 0:128, 256 + 128 * h : 384 + 128 * h].astype(F32) - eks
            inv = tri_scr[n, :, at]
            score = score_scr[n, :, at]
            update = dot_split(inv, beta * target)
            core = eqs + dot_split(score, update)
            writes.append((rk * fading) * update)
            z = att_ref[n, 0:128, 512 + 128 * h : 640 + 128 * h].astype(F32)
            normed = core * lax.rsqrt(jnp.mean(core * core, axis=-1, keepdims=True) + EPS) * gain
            gated_ref[n, :, at] = (normed * (z * jax.nn.sigmoid(z))).astype(BF16)
            inv_high, inv_low = halves(inv)
            tinv_ref[n, :, at] = inv_high
            tinv_ref[n, :, 256 + 128 * h : 384 + 128 * h] = inv_low
            pair_ref[n, :, at] = score.astype(BF16)
            upd_ref[n, :, at] = update.astype(BF16)
            eks_ref[n, :, at] = eks.astype(BF16)
            eqs_ref[n, :, at] = eqs.astype(BF16)
            core_ref[n, :, at] = core.astype(BF16)
        added = dot_exact_left(kt, jnp.concatenate(writes, axis=1))
        ends = jnp.concatenate(
            [jnp.broadcast_to(rows[4 + h : 5 + h, 127:128], (1, dim)) for h in range(2)], axis=1
        )
        state_scr[...] = ends * state + added
        return carry

    lax.fori_loop(0, blocks, advance, 0)


def backward_kernel(
    att_ref, dgated_ref, gain_ref, tinv_ref, pair_ref, upd_ref, eks_ref, eqs_ref, mem_ref, core_ref,
    out_ref,
    rows_scr, cols_scr, dcore_scr, push_scr, dq_state_scr, dtarget_scr, kds_scr, dmem_scr,
    state_scr, colbuf, rowbuf,
):
    blocks = att_ref.shape[0]
    dim = 128
    logits = vectors(att_ref, rows_scr, cols_scr)
    gain = gain_ref[...]
    within = triangle((dim, dim))
    strict = triangle((dim, dim), strict=True)

    def local(n, carry):
        q = att_ref[n, 0:128, 0:128]
        cols = cols_scr[n]
        rq = unit_scale(q, dim**-0.5)
        pushed = []
        for h in range(2):
            at = slice(128 * h, 128 * (h + 1))
            rising = cols[:, 4 + h : 5 + h]
            core = core_ref[n, :, at].astype(F32)
            z = att_ref[n, 0:128, 512 + 128 * h : 640 + 128 * h].astype(F32)
            grad = dgated_ref[n, :, at].astype(F32)
            sigma = jax.nn.sigmoid(z)
            inverse_rms = lax.rsqrt(jnp.mean(core * core, axis=-1, keepdims=True) + EPS)
            normed = core * inverse_rms
            out_ref[n, 0:128, 512 + 128 * h : 640 + 128 * h] = (
                grad * normed * gain * (sigma * (1.0 + z * (1.0 - sigma)))
            ).astype(BF16)
            dnormed = grad * gain * (z * sigma)
            dcore = inverse_rms * (
                dnormed - normed * jnp.mean(dnormed * normed, axis=-1, keepdims=True)
            )
            dcore_scr[n, :, at] = dcore
            push_scr[n, :, at] = dot(pair_ref[n, :, at], dcore.astype(BF16), TN)
            pushed.append((rq * rising) * dcore)
        dq_state_scr[n] = dot(q, jnp.concatenate(pushed, axis=1).astype(BF16), TN)
        return carry

    lax.fori_loop(0, blocks, local, 0)
    state_scr[...] = jnp.zeros_like(state_scr)

    def retreat(i, carry):
        n = blocks - 1 - i
        k = att_ref[n, 0:128, 128:256]
        cols = cols_scr[n]
        rows = rows_scr[n]
        rk = unit_scale(k, 1.0)
        state = state_scr[...]
        dmem_scr[n] = state
        read = dot_exact_left(k, state)
        erased = []
        for h in range(2):
            at = slice(128 * h, 128 * (h + 1))
            beta = cols[:, 2 + h : 3 + h]
            rising = cols[:, 4 + h : 5 + h]
            fading = cols[:, 6 + h : 7 + h]
            kds = read[:, at] * (rk * fading)
            kds_scr[n, :, at] = kds
            high, low = halves(push_scr[n, :, at] + kds)
            inv_high = tinv_ref[n, :, at]
            inv_low = tinv_ref[n, :, 256 + 128 * h : 384 + 128 * h]
            dtarget = dot(
                jnp.concatenate([inv_high, inv_low, inv_high], axis=0),
                jnp.concatenate([high, high, low], axis=0),
                TN,
            )
            dtarget_scr[n, :, at] = dtarget
            erased.append((rk * beta * rising) * dtarget)
        kt = jnp.transpose(k)
        ends = jnp.concatenate(
            [jnp.broadcast_to(rows[4 + h : 5 + h, 127:128], (1, dim)) for h in range(2)], axis=1
        )
        state_scr[...] = (
            ends * state + dq_state_scr[n] - dot_exact_left(kt, jnp.concatenate(erased, axis=1))
        )
        return carry

    lax.fori_loop(0, blocks, retreat, 0)
    last = iota((dim, 1), 0) == dim - 1

    def finish(n, carry):
        q = att_ref[n, 0:128, 0:128]
        k = att_ref[n, 0:128, 128:256]
        cols = cols_scr[n]
        rows = rows_scr[n]
        rk = unit_scale(k, 1.0)
        rq = unit_scale(q, dim**-0.5)
        rk_row = jnp.transpose(jnp.broadcast_to(rk, (dim, dim)))
        both = dot(jnp.concatenate([k, q], axis=0), k, NT)
        kk = both[0:128] * (rk * rk_row)
        qk = both[128:256] * (rq * rk_row)
        dqk = jnp.zeros((dim, dim), F32)
        dkk = jnp.zeros((dim, dim), F32)
        read_out = []
        erase = []
        write = []
        for h in range(2):
            at = slice(128 * h, 128 * (h + 1))
            beta = cols[:, 2 + h : 3 + h]
            rising = cols[:, 4 + h : 5 + h]
            fading = cols[:, 6 + h : 7 + h]
            decay = decay_matrix(cols[:, h : h + 1], rows[h : h + 1, :])
            update = upd_ref[n, :, at]
            dcore = dcore_scr[n, :, at]
            dtarget = dtarget_scr[n, :, at]
            kds = kds_scr[n, :, at]
            outer = dot(
                jnp.concatenate([dcore.astype(BF16), dtarget.astype(BF16)], axis=0), update, NT
            )
            dscore = jnp.where(within, outer[0:128], 0.0) * decay
            dlow = jnp.where(strict, -outer[128:256], 0.0) * decay
            dqk = dqk + dscore
            dkk = dkk + dlow * beta
            dlow_kk = dlow * kk
            eks = eks_ref[n, :, at].astype(F32)
            eqs = eqs_ref[n, :, at].astype(F32)
            value = att_ref[n, 0:128, 256 + 128 * h : 384 + 128 * h].astype(F32)
            out_ref[n, 0:128, 256 + 128 * h : 384 + 128 * h] = (beta * dtarget).astype(BF16)
            dbeta = jnp.sum(dtarget * (value - eks) + dlow_kk, axis=-1, keepdims=True)
            flow = dscore * qk + dlow_kk * beta
            kept = update.astype(F32) * kds
            from_write = jnp.sum(kept, axis=-1, keepdims=True)
            through = jnp.sum(
                mem_ref[n, :, at].astype(F32) * dmem_scr[n, :, at], keepdims=True
            ) * rows[4 + h : 5 + h, 127:128]
            dlog = (
                jnp.sum(flow + dcore * eqs - (beta * dtarget) * eks, axis=-1, keepdims=True)
                - from_write
            )
            dlog = dlog + jnp.where(last, jnp.sum(from_write, keepdims=True) + through, 0.0)
            colbuf[n, :, h : h + 1] = dlog
            colbuf[n, :, 2 + h : 3 + h] = dbeta
            rowbuf[n, h : h + 1, :] = -jnp.sum(flow, axis=0, keepdims=True)
            read_out.append(rising * dcore)
            erase.append((-(beta * rising)) * dtarget)
            write.append(fading * update.astype(F32))
        mem = mem_ref[n]
        top = jnp.concatenate(
            [jnp.concatenate(read_out, axis=1), jnp.concatenate(erase, axis=1)], axis=0
        ).astype(BF16)
        from_mem = dot(top, mem, NT)
        dk = from_mem[128:256] + dot(
            jnp.concatenate(write, axis=1).astype(BF16), dmem_scr[n].astype(BF16), NT
        )
        dq = from_mem[0:128] + dot((dqk * rk_row).astype(BF16), k)
        dk = dk + dot((dqk * rq).astype(BF16), q, TN)
        dk = dk + dot(((dkk + jnp.transpose(dkk)) * rk_row).astype(BF16), k)
        qf = q.astype(F32)
        kf = k.astype(F32)
        dq = rq * (dq - qf * ((rq * rq * dim) * jnp.sum(qf * dq, axis=-1, keepdims=True)))
        dk = rk * (dk - kf * ((rk * rk) * jnp.sum(kf * dk, axis=-1, keepdims=True)))
        out_ref[n, 0:128, 0:128] = dq.astype(BF16)
        out_ref[n, 0:128, 128:256] = dk.astype(BF16)
        return carry

    colbuf[...] = jnp.zeros_like(colbuf)
    rowbuf[...] = jnp.zeros_like(rowbuf)
    lax.fori_loop(0, blocks, finish, 0)
    cols = jnp.concatenate(
        [colbuf[n, :, 0:8] for n in range(blocks)]
        + [jnp.zeros((dim, dim - 8 * blocks), F32)],
        axis=1,
    )
    grads = jnp.transpose(cols)[0 : 8 * blocks] + jnp.concatenate(
        [rowbuf[n] for n in range(blocks)], axis=0
    )
    kind = iota(grads.shape, 0) % 8
    after = mask01(iota((dim, dim), 0) >= iota((dim, dim), 1))
    sigma = jax.nn.sigmoid(logits)
    grads = jnp.where(
        kind < 2, -dot_ones(grads, after) * sigma, grads * sigma * (1.0 - sigma)
    ).astype(BF16)
    for n in range(blocks):
        out_ref[n, 128:136, 0:128] = grads[8 * n : 8 * (n + 1)]
        out_ref[n, 128:136, 128:768] = jnp.zeros((8, 640), BF16)


def sum_kernel(in_ref, out_ref):
    out_ref[...] = jnp.sum(in_ref[...].astype(F32), axis=0)


def shape(dims, dtype=BF16):
    return jax.ShapeDtypeStruct(dims, dtype)


def vmem_call(kernel, outs, scratch=(), flops=0, moved=0, limit=56):
    return pl.pallas_call(
        kernel,
        out_shape=outs,
        scratch_shapes=list(scratch),
        compiler_params=params(limit),
        cost_estimate=pl.CostEstimate(flops=flops, bytes_accessed=moved, transcendentals=0),
    )


def run_forward(att, gain):
    blocks = att.shape[0]
    square = (blocks, 128, 256)
    return vmem_call(
        forward_kernel,
        [shape(square), shape((blocks, 128, 512))] + [shape(square)] * 6,
        [
            pltpu.VMEM((blocks, 8, 128), F32),
            pltpu.VMEM((blocks, 128, 128), F32),
            pltpu.VMEM(square, F32),
            pltpu.VMEM(square, F32),
            pltpu.VMEM((128, 256), F32),
        ],
        flops=12 * 10**9,
        moved=8 * MIB,
    )(att, gain)


def run_backward(att, dgated, gain, saved):
    blocks = att.shape[0]
    square = (blocks, 128, 256)
    return vmem_call(
        backward_kernel,
        shape((blocks, 136, 768)),
        [pltpu.VMEM((blocks, 8, 128), F32), pltpu.VMEM((blocks, 128, 128), F32)]
        + [pltpu.VMEM(square, F32)] * 6
        + [
            pltpu.VMEM((128, 256), F32),
            pltpu.VMEM((blocks, 128, 128), F32),
            pltpu.VMEM((blocks, 8, 128), F32),
        ],
        flops=12 * 10**9,
        moved=8 * MIB,
    )(att, dgated, gain, *saved)


def body(
    hidden_in, grad_out, post_gain, route_ids, route_weight, gate_up, down_proj,
    query_in, key_in, value_in, gate_in, decay_logit, beta_logit, head_gain, out_proj,
):
    ctx = lax.axis_size("ctx")
    exp = lax.axis_size("exp")
    devices = ctx * exp
    tokens, width = hidden_in.shape[1:]
    hidden_units = down_proj.shape[1]
    slots = 4 * devices
    hidden = hidden_in[0]
    grad = grad_out[0]
    gain = post_gain.reshape(1, width)
    ids = route_ids[0]

    steps = 4
    whole = lambda *dims: pl.BlockSpec(dims, lambda i: (0,) * len(dims))
    rows = pl.pallas_call(
        dispatch_kernel,
        grid=(steps,),
        in_specs=[
            whole(tokens, width), whole(tokens, width), whole(1, width),
            whole(*ids.shape), whole(*ids.shape),
        ],
        out_specs=pl.BlockSpec((2 * slots, width // steps), lambda i: (0, i)),
        out_shape=shape((2 * slots, width)),
        scratch_shapes=[
            pltpu.VMEM((2 * tokens, width), BF16),
            pltpu.VMEM((2 * slots, 2 * tokens), BF16),
            pltpu.VMEM((2 * slots, 1), F32),
        ],
        compiler_params=params(),
        cost_estimate=pl.CostEstimate(flops=10**9, bytes_accessed=6 * MIB, transcendentals=0),
    )(hidden, grad, gain, ids, route_weight[0])
    got = lax.all_to_all(
        rows.reshape(devices, 8, width), ("ctx", "exp"), split_axis=0, concat_axis=0, tiled=True
    ).reshape(2 * slots, width)

    packed = vmem_call(pack_kernel, shape((ctx, 136, 768)), moved=4 * MIB)(
        query_in[0], key_in[0], value_in[0], gate_in[0], decay_logit[0], beta_logit[0]
    )
    att = lax.all_to_all(packed, "ctx", split_axis=0, concat_axis=0, tiled=True)
    proj_all = lax.all_gather(out_proj, "ctx", axis=0, tiled=False)

    gain_heads = head_gain.reshape(1, 128)
    gated, *saved = run_forward(att, gain_heads)

    got, gated, saved = lax.optimization_barrier((got, gated, saved))
    back, rows_in, rows_grad, act, gproj = pl.pallas_call(
        expert_kernel,
        in_specs=[
            pl.BlockSpec(memory_space=pltpu.VMEM),
            pl.BlockSpec(memory_space=pl.ANY),
            pl.BlockSpec(memory_space=pl.ANY),
        ],
        out_shape=[
            shape((2 * slots, width // 2)), shape((slots, width)), shape((slots, width)),
            shape((slots, hidden_units)), shape((slots, 2 * hidden_units)),
        ],
        scratch_shapes=[
            pltpu.VMEM((width, 2 * hidden_units), BF16),
            pltpu.VMEM((hidden_units, width), BF16),
            pltpu.SemaphoreType.DMA((2,)),
        ],
        compiler_params=params(),
        cost_estimate=pl.CostEstimate(
            flops=6 * 10**9, bytes_accessed=18 * MIB, transcendentals=0
        ),
    )(got, gate_up[0], down_proj[0])
    returned = lax.all_to_all(
        back.reshape(devices, 8, width // 2), ("ctx", "exp"), split_axis=0, concat_axis=0, tiled=True
    ).reshape(2 * slots, width // 2)
    grad_gate_up = dot(rows_in, gproj, TN).astype(BF16)
    grad_down = dot(act, rows_grad, TN).astype(BF16)
    returned, grad_gate_up, grad_down = lax.optimization_barrier(
        (returned, grad_gate_up, grad_down)
    )

    grad_hidden, dgated = pl.pallas_call(
        combine_kernel,
        grid=(ctx,),
        in_specs=[
            whole(2 * slots, width // 2), whole(tokens, width), whole(tokens, width),
            whole(1, width), whole(*ids.shape),
            pl.BlockSpec((1, width, 256), lambda i: (i, 0, 0)),
        ],
        out_specs=[whole(tokens, width), pl.BlockSpec((1, tokens, 256), lambda i: (i, 0, 0))],
        out_shape=[shape((tokens, width)), shape((ctx, tokens, 256))],
        compiler_params=params(),
        cost_estimate=pl.CostEstimate(flops=2 * 10**9, bytes_accessed=13 * MIB, transcendentals=0),
    )(returned, hidden, grad, gain, ids, proj_all)
    dgated = lax.all_to_all(dgated, "ctx", split_axis=0, concat_axis=0, tiled=True)
    hidden_all = lax.all_gather(grad_hidden, "ctx", axis=0, tiled=True)

    grads = run_backward(att, dgated, gain_heads, saved)
    grads = lax.all_to_all(grads, "ctx", split_axis=0, concat_axis=0, tiled=True)

    scale = float(tokens * devices) ** (-0.5)
    term = (scale * dot(hidden_all, gated.reshape(-1, 256), TN)).astype(BF16)
    terms = lax.all_to_all(
        term.reshape(exp, width // exp, 256), "exp", split_axis=0, concat_axis=0, tiled=True
    )
    grad_out_proj = vmem_call(sum_kernel, shape((width // exp, 256), F32), moved=MIB)(terms)

    dq, dk, dv, dz, ddecay, dbeta = vmem_call(
        unpack_kernel,
        [
            shape(query_in.shape[1:]), shape(key_in.shape[1:]), shape(value_in.shape[1:]),
            shape(gate_in.shape[1:]), shape(decay_logit.shape[1:]), shape(beta_logit.shape[1:]),
        ],
        moved=4 * MIB,
    )(grads)
    return (
        grad_hidden[None], dq[None], dk[None], dv[None], dz[None], ddecay[None], dbeta[None],
        grad_gate_up[None], grad_down[None], grad_out_proj,
    )


def solution(mesh):
    tokens = P("exp", "ctx", None)
    experts = P(("ctx", "exp"), None, None)
    return jax.shard_map(
        body,
        mesh=mesh,
        in_specs=(
            tokens, tokens, P(), tokens, tokens, experts, experts,
            tokens, tokens, tokens, tokens, tokens, tokens, P(), P(None, "ctx"),
        ),
        out_specs=(
            tokens, tokens, tokens, tokens, tokens, tokens, tokens,
            experts, experts, P("exp", "ctx"),
        ),
        check_vma=False,
    )
```

time: 1020 us -> 285 us (0.28)
  other arithmetic: 446 us -> 0 us
  matrix products: 234 us -> 13.3 us
  local copies, waits for them, and re-layouts: 188 us -> 10.7 us
  Pallas kernels: 0 us -> 96.5 us
  waiting for transfers between devices: 40.7 us -> 97.1 us
  starting transfers between devices: 86.3 us -> 32.2 us
  blocking collectives: 0 us -> 19.3 us
    another operation x95 -> x0, other arithmetic: 338 us -> none  [the longest x64 325 us: block_step(): lax.linalg.triangular_solve(system, target, left_side=True, lower=True, u...]
    dot_general x159 -> x3, matrix products: 210 us -> 13.3 us  [dot(): return lax.dot_general(a, b, dims, preferred_element_type=F32)]
    pallas_call x0 -> x8, Pallas kernels: none -> 96.5 us  [the longest x1 36.5 us: run_forward(): vmem_call(forward_kernel, [shape(square), shape((blocks, 128, 512))] + [s...]
    all_to_all x15 -> x5, waiting for transfers between devices: 40.7 us -> 96.4 us  [the longest x1 27.7 us: body(): att = lax.all_to_all(packed, 'ctx', split_axis=0, concat_axis=0, tiled=True)]
    all_to_all x15 -> x5, starting transfers between devices: 85.9 us -> 31.9 us  [the longest x1 11.1 us: body(): lax.all_to_all(rows.reshape(devices, 8, width), ('ctx', 'exp'), split_axi...]
    unnamed x13 -> x0, other arithmetic: 46.4 us -> none
    unnamed x113 -> x26, local copies, waits for them, and re-layouts: 37.4 us -> 10.7 us
    reduce_sum x34 -> x0, other arithmetic: 25.8 us -> none  [the longest x1 9.87 us: body(): moe_grad = jnp.sum(slot_back, axis=1)]
  transfers between devices with their start and end apart: 17 -> 7, of which waited for: 6 -> 5; matrix products, arithmetic and copies ran while one was open for 48% -> 7% of each run, Pallas kernels for 0% -> 30%
where the time goes in v1:
time: 285 us; the launch traced here: 283 us
  waiting for transfers between devices  97.1 us (34%)
  Pallas kernels  96.5 us (34%)
  starting transfers between devices  32.2 us (11%)
  blocking collectives  19.3 us (7%)
  between operations  14.1 us (5%)
  matrix products  13.3 us (5%)
  local copies, waits for them, and re-layouts  10.7 us (4%)
    pallas_call x1, Pallas kernels, run_forward(): vmem_call(forward_kernel, [shape(square), shape((blocks, 128, 512))] + [s...  36.5 us
    all_to_all x1, waiting for transfers between devices, body(): att = lax.all_to_all(packed, 'ctx', split_axis=0, concat_axis=0, tiled=True)  27.7 us
    pallas_call x1, Pallas kernels, run_backward(): vmem_call(backward_kernel, shape((blocks, 136, 768)), [pltpu.VMEM((blocks...  21.7 us
    all_to_all x1, waiting for transfers between devices, body(): lax.all_to_all(rows.reshape(devices, 8, width), ('ctx', 'exp'), split_axi...  20.7 us
    all_to_all x1, waiting for transfers between devices, body(): lax.all_to_all(back.reshape(devices, 8, width // 2), ('ctx', 'exp'), spli...  20.3 us
    all_to_all x1, blocking collectives, body(): lax.all_to_all(dgated, 'ctx', split_axis=0, concat_axis=0, tiled=True)  19.3 us
    all_to_all x1, waiting for transfers between devices, body(): lax.all_to_all(grads, 'ctx', split_axis=0, concat_axis=0, tiled=True)  17.3 us
    pallas_call x1, Pallas kernels, body(): pl.pallas_call(expert_kernel, in_specs=[pl.BlockSpec(memory_space=pltpu.V...  14.8 us
  transfers between devices with their start and end apart: 7, of which 5 were waited for; matrix products, arithmetic and copies ran while one was open for 7% of the time, Pallas kernels for 30%

profile of v1, /device:TPU:1, one launch (start us, length us, event | category | flops | bytes accessed | tf_op | source)
XLA Modules:
  0.0 283.1 jit_solution(8371727737507071864)
XLA Ops:
  7.2 0.7 all-gather.6.cloned.1.call-update
  7.9 1.4 copy.27
  9.3 1.4 copy.28
  10.7 2.7 shard_map.223
  13.4 5.9 %all-to-all-start.1 = ((bf16[8,136,768]{2,1,0:T(8,128)(2,1)}), bf16[8,136,768]{2,1,0:T(8,128)(2,1)S(1)}, u32[]{:S(2)}, u32[]{:S(2)}) async-start(bf16[8,136,768]{2,1,0:T(8,128)(2,1)} %shard_map.223), calls=%async_computation.1 | async-start | bytes 3342336 | tf_op jit(solution)/shard_map/all_to_all | solution.py:641
  19.4 0.7 copy.25
  20.1 0.7 copy.26
  20.9 5.9 %shard_map.222 = bf16[1024,2048]{1,0:T(8,128)(2,1)} custom-call(bf16[128,2048]{1,0:T(8,128)(2,1)} %bitcast.40, bf16[128,2048]{1,0:T(8,128)(2,1)} %bitcast.42, f32[1,2048]{1,0:T(1,128)} %bitcast.55, s32[128,10]{1,0:T(8,128)} %bitcast.45, f32[128,10]{1,0:T(8,128)} %bitcast.50), custom_call_target="tpu_custom_call" | custom-call | flops 1000000000 | bytes 6291456 | tf_op jit(solution)/shard_map/pallas_call | solution.py:617
  26.8 27.7 %all-to-all-done.1.att_ref = bf16[8,136,768]{2,1,0:T(8,128)(2,1)S(1)} async-done(((bf16[8,136,768]{2,1,0:T(8,128)(2,1)}), bf16[8,136,768]{2,1,0:T(8,128)(2,1)S(1)}, u32[]{:S(2)}, u32[]{:S(2)}) %all-to-all-start.1) | async-done | bytes 1671200 | tf_op jit(solution)/shard_map/all_to_all | solution.py:641
  54.5 1.2 copy-done.3
  55.7 11.1 %all-to-all-start = ((bf16[128,8,2048]{2,1,0:T(8,128)(2,1)}), bf16[128,8,2048]{2,1,0:T(8,128)(2,1)}, u32[]{:S(2)}, u32[]{:S(2)}) async-start(bf16[128,8,2048]{2,1,0:T(8,128)(2,1)} %bitcast.36), calls=%async_computation | async-start | bytes 8388608 | tf_op jit(solution)/shard_map/all_to_all | solution.py:634
  66.8 36.5 %shard_map.224 = (bf16[8,128,256]{2,1,0:T(8,128)(2,1)}, bf16[8,128,512]{2,1,0:T(8,128)(2,1)}, bf16[8,128,256]{2,1,0:T(8,128)(2,1)}, bf16[8,128,256]{2,1,0:T(8,12...) custom-call(bf16[8,136,768]{2,1,0:T(8,128)(2,1)} %copy-done.3, ...), custom_call_target="tpu_custom_call" | custom-call | flops 12000000000 | bytes 8388608 | tf_op jit(solution)/shard_map/pallas_call | solution.py:567
  103.3 20.7 %all-to-all-done = bf16[128,8,2048]{2,1,0:T(8,128)(2,1)} async-done(((bf16[128,8,2048]{2,1,0:T(8,128)(2,1)}), bf16[128,8,2048]{2,1,0:T(8,128)(2,1)}, u32[]{:S(2)}, u32[]{:S(2)}) %all-to-all-start) | async-done | bytes 4194336 | tf_op jit(solution)/shard_map/all_to_all | solution.py:634
  124.0 14.8 %shard_map.225 = (bf16[1024,1024]{1,0:T(8,128)(2,1)}, bf16[512,2048]{1,0:T(8,128)(2,1)}, bf16[512,2048]{1,0:T(8,128)(2,1)}, bf16[512,512]{1,0:T(8,128)(2,1)}, bf16[512,1024]{1,0:T(8,128)(2,1)}) custom-call(bf16[1024,2048]{1,0:T(8,128)(2,1)} %bitcast.6.got_ref, bf16[2048,1024]{1,0:T(8,128)(2,1)} %bitcast.59, bf16[512,2048]{1,0:T(8,128)(2,1)} %bitcast.60), custom_call_target="tpu_custom_call" | custom-call | flops 6000000000 | bytes 18874368 | tf_op jit(solution)/shard_map/pallas_call | solution.py:648
  138.8 5.9 %all-to-all-start.2 = ((bf16[128,8,1024]{2,1,0:T(8,128)(2,1)}), bf16[128,8,1024]{2,1,0:T(8,128)(2,1)S(1)}, u32[]{:S(2)}, u32[]{:S(2)}) async-start(bf16[128,8,1024]{2,1,0:T(8,128)(2,1)} %bitcast.39), calls=%async_computation.2 | async-start | bytes 4194304 | tf_op jit(solution)/shard_map/all_to_all | solution.py:669
  144.9 4.3 %convolution_convert_fusion.1 = bf16[512,2048]{1,0:T(8,128)(2,1)} fusion(bf16[512,512]{1,0:T(8,128)(2,1)S(1)} %copy-done.7, bf16[512,2048]{1,0:T(8,128)(2,1)} %get-tuple-element.56), kind=kOutput, calls=%fused_computation.1 | convolution fusion | flops 1074790400 | bytes 4718592 | tf_op jit(solution)/shard_map/dot_general | solution.py:21
  149.3 4.4 %convolution_convert_fusion = bf16[2048,1024]{1,0:T(8,128)(2,1)} fusion(bf16[512,2048]{1,0:T(8,128)(2,1)S(1)} %copy-done.8, bf16[512,1024]{1,0:T(8,128)(2,1)S(1)} %copy-done.9), kind=kOutput, calls=%fused_computation | convolution fusion | flops 2149580800 | bytes 7340032 | tf_op jit(solution)/shard_map/dot_general | solution.py:21
  153.7 20.3 %all-to-all-done.2 = bf16[128,8,1024]{2,1,0:T(8,128)(2,1)S(1)} async-done(((bf16[128,8,1024]{2,1,0:T(8,128)(2,1)}), bf16[128,8,1024]{2,1,0:T(8,128)(2,1)S(1)}, u32[]{:S(2)}, u32[]{:S(2)}) %all-to-all-start.2) | async-done | bytes 2097184 | tf_op jit(solution)/shard_map/all_to_all | solution.py:669
  173.9 1.4 copy-done
  175.3 10.2 %shard_map.226 = (bf16[128,2048]{1,0:T(8,128)(2,1)}, bf16[8,128,256]{2,1,0:T(8,128)(2,1)}) custom-call(bf16[1024,1024]{1,0:T(8,128)(2,1)} %bitcast.37, bf16[128,2048]{1,0:T(8,128)(2,1)} %bitcast.41, bf16[128,2048]{1,0:T(8,128)(2,1)} %bitcast.43, f32[1,2048]{1,0:T(1,128)} %bitcast.56, s32[128,10]{1,0:T(8,128)} %bitcast.46, bf16[8,2048,256]{2,1,0:T(8,128)(2,1)} %bitcast.38), custom_call_target="tpu_custom_call" | custom-call | flops 2000000000 | bytes 13631488 | tf_op jit(solution)/shard_map/pallas_call | solution.py:678
  185.5 19.3 %all_to_all.30.dgated_ref = bf16[8,128,256]{2,1,0:T(8,128)(2,1)} all-to-all(bf16[8,128,256]{2,1,0:T(8,128)(2,1)} %get-tuple-element.59), channel_id=1, replica_groups=mesh['ctx'=8,'exp'=16] {'ctx'}, dimensions={0} | all-to-all | bytes 1048576 | tf_op jit(solution)/shard_map/all_to_all | solution.py:691
  204.8 21.7 %shard_map.227 = bf16[8,136,768]{2,1,0:T(8,128)(2,1)} custom-call(bf16[8,136,768]{2,1,0:T(8,128)(2,1)} %copy-done.3, bf16[8,128,256]{2,1,0:T(8,128)(2,1)} %all_to_all.30.dgated_ref, f32[1,128]{1,0:T(1,128)} %bitcast.66, bf16[8,128,512]{2,1,0:T(8,128)(2,1)} %get-tuple-element.60.tinv_ref, bf16[8,128,256]{2,1,0:T(8,128)(2,1)} %get-tuple-element.61.pair_ref, ...), custom_call_target="tpu_custom_call" | custom-call | flops 12000000000 | bytes 8388608 | tf_op jit(solution)/shard_map/pallas_call | solution.py:585
  226.4 5.4 %all-to-all-start.4 = ((bf16[8,136,768]{2,1,0:T(8,128)(2,1)}), bf16[8,136,768]{2,1,0:T(8,128)(2,1)S(1)}, u32[]{:S(2)}, u32[]{:S(2)}) async-start(bf16[8,136,768]{2,1,0:T(8,128)(2,1)} %shard_map.227), calls=%async_computation.4 | async-start | bytes 3342336 | tf_op jit(solution)/shard_map/all_to_all | solution.py:695
  231.8 4.5 %fusion = bf16[2048,256]{1,0:T(8,128)(2,1)} fusion(bf16[1024,2048]{1,0:T(8,128)(2,1)} %all-gather.4.cloned.1.call-done, bf16[1024,256]{1,0:T(8,128)(2,1)S(1)} %bitcast.69), kind=kOutput, calls=%fused_computation.3 | convolution fusion | flops 1074790400 | bytes 5767168 | tf_op jit(solution)/shard_map/dot_general | solution.py:21
  236.3 17.3 %all-to-all-done.4.in_ref = bf16[8,136,768]{2,1,0:T(8,128)(2,1)S(1)} async-done(((bf16[8,136,768]{2,1,0:T(8,128)(2,1)}), bf16[8,136,768]{2,1,0:T(8,128)(2,1)S(1)}, u32[]{:S(2)}, u32[]{:S(2)}) %all-to-all-start.4) | async-done | bytes 1671200 | tf_op jit(solution)/shard_map/all_to_all | solution.py:695
  253.6 3.7 %all-to-all-start.5 = ((bf16[16,128,256]{2,1,0:T(8,128)(2,1)}), bf16[16,128,256]{2,1,0:T(8,128)(2,1)S(1)}, u32[]{:S(2)}, u32[]{:S(2)}) async-start(bf16[16,128,256]{2,1,0:T(8,128)(2,1)} %bitcast.44), calls=%async_computation.5 | async-start | bytes 2097152 | tf_op jit(solution)/shard_map/all_to_all | solution.py:699
  257.3 2.7 shard_map.228
  260.0 1.4 copy.29
  261.4 1.4 copy.30
  262.8 10.5 %all-to-all-done.5.in_ref = bf16[16,128,256]{2,1,0:T(8,128)(2,1)S(1)} async-done(((bf16[16,128,256]{2,1,0:T(8,128)(2,1)}), bf16[16,128,256]{2,1,0:T(8,128)(2,1)S(1)}, u32[]{:S(2)}, u32[]{:S(2)}) %all-to-all-start.5) | async-done | bytes 1048608 | tf_op jit(solution)/shard_map/all_to_all | solution.py:699
  273.3 1.0 copy-done.2
  274.3 2.0 shard_map.229
  (22 shorter events, 0.3 us)
Async XLA Ops:
  7.2 166.7 %all-gather.6.cloned.1.call-start = ((), (), s32[]{:S(2)}) async-start(), calls=%async_computation.7 | async-start | bytes 9437184 | tf_op jit(solution)/shard_map/all_gather | solution.py:642
  13.4 5.9 %copy-start.4 = (s32[1,128,10]{1,0,2:T(1,128)S(1)}, s32[1,128,10]{1,0,2:T(1,128)}, u32[]{:S(2)}) copy-start(s32[1,128,10]{1,0,2:T(1,128)} %param.18) | copy-start | bytes 15364
  13.4 6.7 %copy-start.5 = (f32[1,128,10]{1,0,2:T(1,128)S(1)}, f32[1,128,10]{1,0,2:T(1,128)}, u32[]{:S(2)}) copy-start(f32[1,128,10]{1,0,2:T(1,128)} %param.19) | copy-start | bytes 15364
  13.4 41.1 %all-to-all-start.1 = ((bf16[8,136,768]{2,1,0:T(8,128)(2,1)}), bf16[8,136,768]{2,1,0:T(8,128)(2,1)S(1)}, u32[]{:S(2)}, u32[]{:S(2)}) async-start(bf16[8,136,768]{2,1,0:T(8,128)(2,1)} %shard_map.223), calls=%async_computation.1 | async-start | bytes 3342336 | tf_op jit(solution)/shard_map/all_to_all | solution.py:641
  54.5 1.2 copy-start.3
  55.7 68.2 %all-to-all-start = ((bf16[128,8,2048]{2,1,0:T(8,128)(2,1)}), bf16[128,8,2048]{2,1,0:T(8,128)(2,1)}, u32[]{:S(2)}, u32[]{:S(2)}) async-start(bf16[128,8,2048]{2,1,0:T(8,128)(2,1)} %bitcast.36), calls=%async_computation | async-start | bytes 8388608 | tf_op jit(solution)/shard_map/all_to_all | solution.py:634
  138.8 6.1 %copy-start.7 = (bf16[512,512]{1,0:T(8,128)(2,1)S(1)}, bf16[512,512]{1,0:T(8,128)(2,1)}, u32[]{:S(2)}) copy-start(bf16[512,512]{1,0:T(8,128)(2,1)} %get-tuple-element.55) | copy-start | bytes 1572868
  138.8 35.1 %all-to-all-start.2 = ((bf16[128,8,1024]{2,1,0:T(8,128)(2,1)}), bf16[128,8,1024]{2,1,0:T(8,128)(2,1)S(1)}, u32[]{:S(2)}, u32[]{:S(2)}) async-start(bf16[128,8,1024]{2,1,0:T(8,128)(2,1)} %bitcast.39), calls=%async_computation.2 | async-start | bytes 4194304 | tf_op jit(solution)/shard_map/all_to_all | solution.py:669
  144.6 87.1 %all-gather.4.cloned.1.call-start = ((), (), s32[]{:S(2)}) async-start(), calls=%async_computation.6 | async-start | bytes 4718592 | tf_op jit(solution)/shard_map/all_gather | solution.py:692
  144.9 4.4 %copy-start.8 = (bf16[512,2048]{1,0:T(8,128)(2,1)S(1)}, bf16[512,2048]{1,0:T(8,128)(2,1)}, u32[]{:S(2)}) copy-start(bf16[512,2048]{1,0:T(8,128)(2,1)} %get-tuple-element.53) | copy-start | bytes 6291460
  144.9 4.4 %copy-start.9 = (bf16[512,1024]{1,0:T(8,128)(2,1)S(1)}, bf16[512,1024]{1,0:T(8,128)(2,1)}, u32[]{:S(2)}) copy-start(bf16[512,1024]{1,0:T(8,128)(2,1)} %get-tuple-element.54) | copy-start | bytes 3145732
  173.9 1.4 copy-start
  226.4 5.4 %copy-start.6 = (bf16[8,128,256]{2,1,0:T(8,128)(2,1)S(1)}, bf16[8,128,256]{2,1,0:T(8,128)(2,1)}, u32[]{:S(2)}) copy-start(bf16[8,128,256]{2,1,0:T(8,128)(2,1)} %get-tuple-element.75) | copy-start | bytes 1572868
  226.4 27.2 %all-to-all-start.4 = ((bf16[8,136,768]{2,1,0:T(8,128)(2,1)}), bf16[8,136,768]{2,1,0:T(8,128)(2,1)S(1)}, u32[]{:S(2)}, u32[]{:S(2)}) async-start(bf16[8,136,768]{2,1,0:T(8,128)(2,1)} %shard_map.227), calls=%async_computation.4 | async-start | bytes 3342336 | tf_op jit(solution)/shard_map/all_to_all | solution.py:695
  253.6 3.7 %copy-start.1 = (bf16[8,136,768]{2,1,0:T(8,128)(2,1)}, bf16[8,136,768]{2,1,0:T(8,128)(2,1)S(1)}, u32[]{:S(2)}) copy-start(bf16[8,136,768]{2,1,0:T(8,128)(2,1)S(1)} %all-to-all-done.4.in_ref) | copy-start | bytes 5013508
  253.6 19.7 %all-to-all-start.5 = ((bf16[16,128,256]{2,1,0:T(8,128)(2,1)}), bf16[16,128,256]{2,1,0:T(8,128)(2,1)S(1)}, u32[]{:S(2)}, u32[]{:S(2)}) async-start(bf16[16,128,256]{2,1,0:T(8,128)(2,1)} %bitcast.44), calls=%async_computation.5 | async-start | bytes 2097152 | tf_op jit(solution)/shard_map/all_to_all | solution.py:699
  273.3 1.0 copy-start.2
Sparse Core Ops, SparseCore 0:
  9.7 77.7 all-gather.5
  185.6 33.7 all-gather.3

commit v2 on v1

--- a/solution.py
+++ b/solution.py
@@ -11,6 +11,7 @@
 BF16 = jnp.bfloat16
 EPS = 1e-6
 MIB = 1 << 20
+INVERSE_GROUP = 4
 
 NN = (((1,), (0,)), ((), ()))
 NT = (((1,), (1,)), ((), ()))
@@ -61,7 +62,7 @@
 
 def pack_kernel(q_ref, k_ref, v_ref, z_ref, decay_ref, beta_ref, out_ref):
     groups = out_ref.shape[0]
-    heads = decay_ref.shape[1]
+    heads = decay_ref.shape[0]
     row = iota((8 * groups, heads), 0)
     head = iota((8 * groups, heads), 1)
     kind = row % 8
@@ -69,7 +70,7 @@
     is_beta = (kind == 2) | (kind == 3)
     pick_decay = mask01((head == own) & ~is_beta)
     pick_beta = mask01((head == own) & is_beta)
-    rows = dot(pick_decay, decay_ref[...], NT) + dot(pick_beta, beta_ref[...], NT)
+    rows = dot(pick_decay, decay_ref[...]) + dot(pick_beta, beta_ref[...])
     rows = rows.astype(BF16)
     for i in range(groups):
         out_ref[i, 0:128, 0:128] = q_ref[:, 128 * i : 128 * (i + 1)]
@@ -82,7 +83,7 @@
 
 def unpack_kernel(in_ref, q_ref, k_ref, v_ref, z_ref, decay_ref, beta_ref):
     groups = in_ref.shape[0]
-    heads = decay_ref.shape[1]
+    heads = decay_ref.shape[0]
     rows = []
     for i in range(groups):
         q_ref[:, 128 * i : 128 * (i + 1)] = in_ref[i, 0:128, 0:128]
@@ -91,27 +92,27 @@
         z_ref[:, 256 * i : 256 * (i + 1)] = in_ref[i, 0:128, 512:768]
         rows.append(in_ref[i, 128:136, 0:128].astype(F32))
     rows = jnp.concatenate(rows, axis=0).astype(BF16)
-    row = iota((8 * groups, heads), 0)
-    head = iota((8 * groups, heads), 1)
+    row = iota((heads, 8 * groups), 1)
+    head = iota((heads, 8 * groups), 0)
     kind = row % 8
     own = 2 * (row // 8) + kind % 2
-    decay_ref[...] = dot(rows, mask01((head == own) & (kind < 2)), TN).astype(BF16)
-    beta_ref[...] = dot(rows, mask01((head == own) & ((kind == 2) | (kind == 3))), TN).astype(BF16)
+    decay_ref[...] = dot(mask01((head == own) & (kind < 2)), rows).astype(BF16)
+    beta_ref[...] = dot(mask01((head == own) & ((kind == 2) | (kind == 3))), rows).astype(BF16)
 
 
 def slot_code(ids_ref, weight_ref):
-    tokens, top = ids_ref.shape
+    top, _, tokens = ids_ref.shape
     held = 128
-    expert = iota((tokens, held), 1)
-    named = jnp.zeros((tokens, held), F32)
-    weight = jnp.zeros((tokens, held), F32)
+    expert = iota((held, tokens), 0)
+    named = jnp.zeros((held, tokens), F32)
+    weight = jnp.zeros((held, tokens), F32)
     for k in range(top):
-        hit = ids_ref[:, k : k + 1] == expert
+        hit = ids_ref[k] == expert
         named = jnp.where(hit, 1.0, named)
         if weight_ref is not None:
-            weight = jnp.where(hit, weight_ref[:, k : k + 1], weight)
-    earlier = mask01(iota((tokens, tokens), 0) > iota((tokens, tokens), 1))
-    rank = dot(earlier, named.astype(BF16))
+            weight = jnp.where(hit, weight_ref[k], weight)
+    earlier = mask01(iota((tokens, tokens), 0) < iota((tokens, tokens), 1))
+    rank = dot(named.astype(BF16), earlier)
     return jnp.where(named > 0.5, rank, -1.0), weight
 
 
@@ -128,16 +129,16 @@
         both[0:tokens, :] = (hidden * inverse * gain_ref[...]).astype(BF16)
         both[tokens:, :] = grad_ref[...]
         code, weight = slot_code(ids_ref, weight_ref)
-        held = code.shape[1]
+        held = code.shape[0]
         spread = mask01(iota((rows, held), 0) // 8 == iota((rows, held), 1))
-        wide = dot(spread, code.astype(BF16), NT)
+        wide = dot(spread, code.astype(BF16))
         row = iota((rows, tokens), 0) % 8
         hit = wide == (row % 4).astype(F32)
         high = weight.astype(BF16)
         rest = weight - high.astype(F32)
         middle = rest.astype(BF16)
         low = (rest - middle.astype(F32)).astype(BF16)
-        wide_weight = dot(spread, high, NT) + dot(spread, middle, NT) + dot(spread, low, NT)
+        wide_weight = dot(spread, high) + dot(spread, middle) + dot(spread, low)
         is_grad = row >= 4
         pick[:, 0:tokens] = mask01(hit & ~is_grad)
         pick[:, tokens:] = mask01(hit & is_grad)
@@ -209,32 +210,57 @@
     lax.fori_loop(0, width // 512, backward, 0)
 
 
-def combine_kernel(
-    back_ref, hidden_ref, grad_ref, gain_ref, ids_ref, proj_ref, hidden_grad_ref, out_ref
+def combine_kernel(back_ref, hidden_ref, grad_ref, gain_ref, ids_ref, out_ref):
+    tokens, width = hidden_ref.shape
+    code, _ = slot_code(ids_ref, None)
+    held = code.shape[0]
+    code = jnp.transpose(code)
+    rows = 8 * held
+    spread = mask01(iota((held, rows), 0) == iota((held, rows), 1) // 8)
+    wide = dot(code.astype(BF16), spread)
+    place = iota((tokens, rows), 1) % 8
+    hit = wide == (place % 4).astype(F32)
+    first = mask01(hit & (place < 4))
+    second = mask01(hit & (place >= 4))
+    hidden = hidden_ref[...].astype(F32)
+    inverse = lax.rsqrt(jnp.mean(hidden * hidden, axis=-1, keepdims=True) + EPS)
+    moe_grad = jnp.concatenate([dot(first, back_ref[...]), dot(second, back_ref[...])], axis=1)
+    scaled = moe_grad * gain_ref[...]
+    inner = jnp.mean(scaled * hidden, axis=-1, keepdims=True)
+    norm_grad = inverse * scaled - hidden * (inverse * inverse * inverse * inner)
+    out_ref[...] = (grad_ref[...].astype(F32) + norm_grad).astype(BF16)
+
+
+def project_first_kernel(a_ref, b_ref, c_ref, d_ref, proj_ref, gated_ref, grad_ref, term_ref):
+    project((a_ref, b_ref, c_ref, d_ref), proj_ref, gated_ref, 0, grad_ref, None, term_ref, 1.0)
+
+
+def project_last_kernel(
+    a_ref, b_ref, c0_ref, c1_ref, d0_ref, d1_ref, proj_ref, gated_ref, sofar_ref,
+    grad_ref, term_ref, *, scale
 ):
-    tokens, width = hidden_ref.shape
-
-    @pl.when(pl.program_id(0) == 0)
-    def _():
-        code, _ = slot_code(ids_ref, None)
-        held = code.shape[1]
-        rows = 8 * held
-        spread = mask01(iota((held, rows), 0) == iota((held, rows), 1) // 8)
-        wide = dot(code.astype(BF16), spread)
-        place = iota((tokens, rows), 1) % 8
-        hit = wide == (place % 4).astype(F32)
-        first = mask01(hit & (place < 4))
-        second = mask01(hit & (place >= 4))
-        gain = gain_ref[...]
-        hidden = hidden_ref[...].astype(F32)
-        inverse = lax.rsqrt(jnp.mean(hidden * hidden, axis=-1, keepdims=True) + EPS)
-        moe_grad = jnp.concatenate([dot(first, back_ref[...]), dot(second, back_ref[...])], axis=1)
-        scaled = moe_grad * gain
-        inner = jnp.mean(scaled * hidden, axis=-1, keepdims=True)
-        norm_grad = inverse * scaled - hidden * (inverse * inverse * inverse * inner)
-        hidden_grad_ref[...] = (grad_ref[...].astype(F32) + norm_grad).astype(BF16)
-
-    out_ref[0] = dot(hidden_grad_ref[...], proj_ref[0]).astype(BF16)
+    pieces = (a_ref, b_ref, c0_ref, c1_ref, d0_ref, d1_ref)
+    project(pieces, proj_ref, gated_ref, 4, grad_ref, sofar_ref, term_ref, scale)
+
+
+def project(pieces, proj_ref, gated_ref, slot, grad_ref, sofar_ref, term_ref, scale):
+    row = 0
+    for pair in (pieces[:2], pieces[2:]):
+        block = jnp.concatenate([piece[...] for piece in pair], axis=0)
+        out = dot(block, proj_ref[...])
+        for i in range(2):
+            grad_ref[row + i] = out[128 * i : 128 * (i + 1)]
+        row += 2
+    left = jnp.concatenate([gated_ref[slot + i] for i in range(4)], axis=1)
+    for j in range(term_ref.shape[0] // 2):
+        at = slice(256 * j, 256 * (j + 1))
+        right = jnp.concatenate([piece[:, at] for piece in pieces], axis=0)
+        term = dot(left, right)
+        for i in range(2):
+            part = term[:, 128 * i : 128 * (i + 1)]
+            if sofar_ref is not None:
+                part = part + sofar_ref[2 * j + i]
+            term_ref[2 * j + i] = (part * scale).astype(term_ref.dtype)
 
 
 def triangle(shape, strict=False):
@@ -279,7 +305,7 @@
 
 
 def forward_kernel(
-    att_ref, gain_ref,
+    slot_ref, att_ref, gain_ref,
     gated_ref, tinv_ref, pair_ref, upd_ref, eks_ref, eqs_ref, mem_ref, core_ref,
     rows_scr, cols_scr, tri_scr, score_scr, state_scr,
 ):
@@ -290,31 +316,43 @@
     r = iota((dim, dim), 0)
     c = iota((dim, dim), 1)
 
-    def inverse(n, carry):
-        q = att_ref[n, 0:128, 0:128]
-        k = att_ref[n, 0:128, 128:256]
-        rows = rows_scr[n]
-        cols = cols_scr[n]
-        rk = unit_scale(k, 1.0)
-        rq = unit_scale(q, dim**-0.5)
-        rk_row = jnp.transpose(jnp.broadcast_to(rk, (dim, dim)))
-        both = dot(jnp.concatenate([k, q], axis=0), k, NT)
-        kk = both[0:128] * (rk * rk_row)
-        qk = both[128:256] * (rq * rk_row)
-        for h in range(2):
-            decay = decay_matrix(cols[:, h : h + 1], rows[h : h + 1, :])
-            low = jnp.where(strict, cols[:, 2 + h : 3 + h] * decay * kk, 0.0)
-            inv = jnp.where(r == c, 1.0, 0.0) - jnp.where(r // 2 == c // 2, low, 0.0)
-            size = 2
-            while size < dim:
-                level = (r // (2 * size) == c // (2 * size)) & (r // size != c // size)
-                inv = inv - dot_split(dot_split(inv, jnp.where(level, low, 0.0)), inv)
-                size *= 2
-            tri_scr[n, :, 128 * h : 128 * (h + 1)] = inv
-            score_scr[n, :, 128 * h : 128 * (h + 1)] = qk * decay
+    def inverse(i, carry):
+        lows = []
+        scores = []
+        group = [INVERSE_GROUP * i + g for g in range(INVERSE_GROUP)]
+        for n in group:
+            q = att_ref[n, 0:128, 0:128]
+            k = att_ref[n, 0:128, 128:256]
+            rows = rows_scr[n]
+            cols = cols_scr[n]
+            rk = unit_scale(k, 1.0)
+            rq = unit_scale(q, dim**-0.5)
+            rk_row = jnp.transpose(jnp.broadcast_to(rk, (dim, dim)))
+            both = dot(jnp.concatenate([k, q], axis=0), k, NT)
+            kk = both[0:128] * (rk * rk_row)
+            qk = both[128:256] * (rq * rk_row)
+            for h in range(2):
+                decay = decay_matrix(cols[:, h : h + 1], rows[h : h + 1, :])
+                lows.append(jnp.where(strict, cols[:, 2 + h : 3 + h] * decay * kk, 0.0))
+                scores.append(qk * decay)
+        invs = [
+            jnp.where(r == c, 1.0, 0.0) - jnp.where(r // 2 == c // 2, low, 0.0) for low in lows
+        ]
+        size = 2
+        while size < dim:
+            level = (r // (2 * size) == c // (2 * size)) & (r // size != c // size)
+            steps = [
+                dot_split(inv, jnp.where(level, low, 0.0)) for inv, low in zip(invs, lows)
+            ]
+            invs = [inv - dot_split(step, inv) for inv, step in zip(invs, steps)]
+            size *= 2
+        for g, n in enumerate(group):
+            for h in range(2):
+                tri_scr[n, :, 128 * h : 128 * (h + 1)] = invs[2 * g + h]
+                score_scr[n, :, 128 * h : 128 * (h + 1)] = scores[2 * g + h]
         return carry
 
-    lax.fori_loop(0, blocks, inverse, 0)
+    lax.fori_loop(0, blocks // INVERSE_GROUP, inverse, 0)
     state_scr[...] = jnp.zeros_like(state_scr)
     gain = gain_ref[...]
 
@@ -345,7 +383,9 @@
             writes.append((rk * fading) * update)
             z = att_ref[n, 0:128, 512 + 128 * h : 640 + 128 * h].astype(F32)
             normed = core * lax.rsqrt(jnp.mean(core * core, axis=-1, keepdims=True) + EPS) * gain
-            gated_ref[n, :, at] = (normed * (z * jax.nn.sigmoid(z))).astype(BF16)
+            gated_ref[slot_ref[n], at, :] = jnp.transpose(
+                normed * (z * jax.nn.sigmoid(z))
+            ).astype(BF16)
             inv_high, inv_low = halves(inv)
             tinv_ref[n, :, at] = inv_high
             tinv_ref[n, :, 256 + 128 * h : 384 + 128 * h] = inv_low
@@ -365,15 +405,18 @@
 
 
 def backward_kernel(
-    att_ref, dgated_ref, gain_ref, tinv_ref, pair_ref, upd_ref, eks_ref, eqs_ref, mem_ref, core_ref,
+    order_ref, att_ref, first_ref, last_ref, gain_ref, tinv_ref, pair_ref, upd_ref, eks_ref, eqs_ref, mem_ref, core_ref,
     out_ref,
     rows_scr, cols_scr, dcore_scr, push_scr, dq_state_scr, dtarget_scr, kds_scr, dmem_scr,
-    state_scr, colbuf, rowbuf,
+    state_scr, colbuf, rowbuf, dgated_ref,
 ):
     blocks = att_ref.shape[0]
     dim = 128
     logits = vectors(att_ref, rows_scr, cols_scr)
     gain = gain_ref[...]
+    for i in range(4):
+        dgated_ref[order_ref[i]] = first_ref[i]
+        dgated_ref[order_ref[4 + i]] = last_ref[i]
     within = triangle((dim, dim))
     strict = triangle((dim, dim), strict=True)
 
@@ -387,7 +430,7 @@
             rising = cols[:, 4 + h : 5 + h]
             core = core_ref[n, :, at].astype(F32)
             z = att_ref[n, 0:128, 512 + 128 * h : 640 + 128 * h].astype(F32)
-            grad = dgated_ref[n, :, at].astype(F32)
+            grad = dgated_ref[n, :, at]
             sigma = jax.nn.sigmoid(z)
             inverse_rms = lax.rsqrt(jnp.mean(core * core, axis=-1, keepdims=True) + EPS)
             normed = core * inverse_rms
@@ -544,16 +587,24 @@
 
 
 def sum_kernel(in_ref, out_ref):
-    out_ref[...] = jnp.sum(in_ref[...].astype(F32), axis=0)
+    total = jnp.sum(in_ref[...].astype(F32), axis=0)
+    out_ref[...] = jnp.transpose(total)
 
 
 def shape(dims, dtype=BF16):
     return jax.ShapeDtypeStruct(dims, dtype)
 
 
-def vmem_call(kernel, outs, scratch=(), flops=0, moved=0, limit=56):
+def whole(*dims):
+    return pl.BlockSpec(dims, lambda *ids: (0,) * len(dims))
+
+
+def vmem_call(kernel, outs, scratch=(), flops=0, moved=0, limit=56, scalars=0, args=0):
+    specs = [pl.BlockSpec(memory_space=pltpu.SMEM)] * scalars
+    specs += [pl.BlockSpec(memory_space=pltpu.VMEM)] * args
     return pl.pallas_call(
         kernel,
+        in_specs=specs,
         out_shape=outs,
         scratch_shapes=list(scratch),
         compiler_params=params(limit),
@@ -561,12 +612,12 @@
     )
 
 
-def run_forward(att, gain):
+def run_forward(slot, att, gain):
     blocks = att.shape[0]
     square = (blocks, 128, 256)
     return vmem_call(
         forward_kernel,
-        [shape(square), shape((blocks, 128, 512))] + [shape(square)] * 6,
+        [shape((blocks, 256, 128)), shape((blocks, 128, 512))] + [shape(square)] * 6,
         [
             pltpu.VMEM((blocks, 8, 128), F32),
             pltpu.VMEM((blocks, 128, 128), F32),
@@ -574,12 +625,14 @@
             pltpu.VMEM(square, F32),
             pltpu.VMEM((128, 256), F32),
         ],
-        flops=12 * 10**9,
+        flops=4 * 10**9,
         moved=8 * MIB,
-    )(att, gain)
-
-
-def run_backward(att, dgated, gain, saved):
+        scalars=1,
+        args=2,
+    )(slot, att, gain)
+
+
+def run_backward(order, att, first, last, gain, saved):
     blocks = att.shape[0]
     square = (blocks, 128, 256)
     return vmem_call(
@@ -591,30 +644,19 @@
             pltpu.VMEM((128, 256), F32),
             pltpu.VMEM((blocks, 128, 128), F32),
             pltpu.VMEM((blocks, 8, 128), F32),
+            pltpu.VMEM(square, F32),
         ],
-        flops=12 * 10**9,
+        flops=6 * 10**9,
         moved=8 * MIB,
-    )(att, dgated, gain, *saved)
-
-
-def body(
-    hidden_in, grad_out, post_gain, route_ids, route_weight, gate_up, down_proj,
-    query_in, key_in, value_in, gate_in, decay_logit, beta_logit, head_gain, out_proj,
-):
-    ctx = lax.axis_size("ctx")
-    exp = lax.axis_size("exp")
-    devices = ctx * exp
-    tokens, width = hidden_in.shape[1:]
-    hidden_units = down_proj.shape[1]
-    slots = 4 * devices
-    hidden = hidden_in[0]
-    grad = grad_out[0]
-    gain = post_gain.reshape(1, width)
-    ids = route_ids[0]
-
+        scalars=1,
+        args=4 + len(saved),
+    )(order, att, first, last, gain, *saved)
+
+
+def run_dispatch(hidden, grad, gain, ids, weight, slots):
+    tokens, width = hidden.shape
     steps = 4
-    whole = lambda *dims: pl.BlockSpec(dims, lambda i: (0,) * len(dims))
-    rows = pl.pallas_call(
+    return pl.pallas_call(
         dispatch_kernel,
         grid=(steps,),
         in_specs=[
@@ -630,22 +672,14 @@
         ],
         compiler_params=params(),
         cost_estimate=pl.CostEstimate(flops=10**9, bytes_accessed=6 * MIB, transcendentals=0),
-    )(hidden, grad, gain, ids, route_weight[0])
-    got = lax.all_to_all(
-        rows.reshape(devices, 8, width), ("ctx", "exp"), split_axis=0, concat_axis=0, tiled=True
-    ).reshape(2 * slots, width)
-
-    packed = vmem_call(pack_kernel, shape((ctx, 136, 768)), moved=4 * MIB)(
-        query_in[0], key_in[0], value_in[0], gate_in[0], decay_logit[0], beta_logit[0]
-    )
-    att = lax.all_to_all(packed, "ctx", split_axis=0, concat_axis=0, tiled=True)
-    proj_all = lax.all_gather(out_proj, "ctx", axis=0, tiled=False)
-
-    gain_heads = head_gain.reshape(1, 128)
-    gated, *saved = run_forward(att, gain_heads)
-
-    got, gated, saved = lax.optimization_barrier((got, gated, saved))
-    back, rows_in, rows_grad, act, gproj = pl.pallas_call(
+    )(hidden, grad, gain, ids, weight)
+
+
+def run_experts(got, gate_up, down):
+    rows, width = got.shape
+    slots = rows // 2
+    hidden_units = down.shape[0]
+    return pl.pallas_call(
         expert_kernel,
         in_specs=[
             pl.BlockSpec(memory_space=pltpu.VMEM),
@@ -665,52 +699,126 @@
         cost_estimate=pl.CostEstimate(
             flops=6 * 10**9, bytes_accessed=18 * MIB, transcendentals=0
         ),
-    )(got, gate_up[0], down_proj[0])
+    )(got, gate_up, down)
+
+
+def run_combine(returned, hidden, grad, gain, ids):
+    return vmem_call(
+        combine_kernel, shape(hidden.shape), flops=10**9, moved=5 * MIB, limit=48, args=5
+    )(returned, hidden, grad, gain, ids)
+
+
+def block_order(me, ctx):
+    shift = jnp.array([0, 0, ctx - 2, 2, ctx - 2, 2, 4, 4], jnp.int32)
+    flip = jnp.array([0, 1, 0, 0, 1, 1, 0, 1], jnp.int32)
+    order = ((me + shift) % ctx) ^ flip
+    position = lax.iota(jnp.int32, ctx)
+    chip = (position // 2 - me // 2 + ctx // 2) % (ctx // 2)
+    other = (position ^ me) & 1
+    slot = jnp.where(
+        chip == 0, other, jnp.where(chip == 2, 6 + other, jnp.where(chip == 1, 3, 2) + 2 * other)
+    )
+    return order, slot
+
+
+def project_hidden(hidden, proj, gated, scale, ctx, exp):
+    def send(x, step):
+        return lax.ppermute(x, "ctx", [(i, (i + step) % ctx) for i in range(ctx)])
+
+    def swap(x):
+        return lax.ppermute(x, "ctx", [(i, i ^ 1) for i in range(ctx)])
+
+    half = hidden.shape[0] // 2
+    before = send(hidden, 2)
+    after = send(hidden, ctx - 2)
+    mate = swap(hidden)
+    far = [send(before[:half], 2), send(after[half:], ctx - 2)]
+    before_mate = swap(before)
+    after_mate = swap(after)
+    chunks = (exp, 256, hidden.shape[1] // exp)
+    grads = shape((4, 128, 256), F32)
+    first, sofar = vmem_call(
+        project_first_kernel, [grads, shape(chunks, F32)], flops=10**9, moved=6 * MIB,
+        limit=28, args=6,
+    )(hidden, mate, before, after, proj, gated)
+    far_mate = [swap(x) for x in far]
+    last, terms = vmem_call(
+        functools.partial(project_last_kernel, scale=scale),
+        [grads, shape(chunks)],
+        flops=10**9,
+        moved=7 * MIB,
+        limit=28,
+        args=9,
+    )(before_mate, after_mate, *far, *far_mate, proj, gated, sofar)
+    return first, last, terms
+
+
+def body(
+    hidden_in, grad_out, post_gain, route_ids, route_weight, gate_up, down_proj,
+    query_in, key_in, value_in, gate_in, decay_logit, beta_logit, head_gain, out_proj,
+):
+    ctx = lax.axis_size("ctx")
+    exp = lax.axis_size("exp")
+    devices = ctx * exp
+    order, slot = block_order(lax.axis_index("ctx"), ctx)
+    tokens, width = hidden_in.shape[1:]
+    slots = 4 * devices
+    hidden = hidden_in[0]
+    grad = grad_out[0]
+    gain = post_gain.reshape(1, width)
+    gain_heads = head_gain.reshape(1, 128)
+    ids = jnp.transpose(route_ids, (2, 0, 1))
+
+    rows = run_dispatch(
+        hidden, grad, gain, ids, jnp.transpose(route_weight, (2, 0, 1)), slots
+    )
+    got = lax.all_to_all(
+        rows.reshape(devices, 8, width), ("ctx", "exp"), split_axis=0, concat_axis=0, tiled=True
+    ).reshape(2 * slots, width)
+    packed = vmem_call(pack_kernel, shape((ctx, 136, 768)), moved=4 * MIB, limit=12, args=6)(
+        query_in[0], key_in[0], value_in[0], gate_in[0], decay_logit[0].T, beta_logit[0].T
+    )
+
+    got, packed = lax.optimization_barrier((got, packed))
+    att = lax.all_to_all(packed, "ctx", split_axis=0, concat_axis=0, tiled=True)
+    back, rows_in, rows_grad, act, gproj = run_experts(got, gate_up[0], down_proj[0])
+
+    back, att = lax.optimization_barrier((back, att))
     returned = lax.all_to_all(
         back.reshape(devices, 8, width // 2), ("ctx", "exp"), split_axis=0, concat_axis=0, tiled=True
     ).reshape(2 * slots, width // 2)
+    gated, *saved = run_forward(slot, att, gain_heads)
     grad_gate_up = dot(rows_in, gproj, TN).astype(BF16)
     grad_down = dot(act, rows_grad, TN).astype(BF16)
-    returned, grad_gate_up, grad_down = lax.optimization_barrier(
-        (returned, grad_gate_up, grad_down)
-    )
-
-    grad_hidden, dgated = pl.pallas_call(
-        combine_kernel,
-        grid=(ctx,),
-        in_specs=[
-            whole(2 * slots, width // 2), whole(tokens, width), whole(tokens, width),
-            whole(1, width), whole(*ids.shape),
-            pl.BlockSpec((1, width, 256), lambda i: (i, 0, 0)),
-        ],
-        out_specs=[whole(tokens, width), pl.BlockSpec((1, tokens, 256), lambda i: (i, 0, 0))],
-        out_shape=[shape((tokens, width)), shape((ctx, tokens, 256))],
-        compiler_params=params(),
-        cost_estimate=pl.CostEstimate(flops=2 * 10**9, bytes_accessed=13 * MIB, transcendentals=0),
-    )(returned, hidden, grad, gain, ids, proj_all)
-    dgated = lax.all_to_all(dgated, "ctx", split_axis=0, concat_axis=0, tiled=True)
-    hidden_all = lax.all_gather(grad_hidden, "ctx", axis=0, tiled=True)
-
-    grads = run_backward(att, dgated, gain_heads, saved)
+    returned, gated, saved, grad_gate_up, grad_down = lax.optimization_barrier(
+        (returned, gated, saved, grad_gate_up, grad_down)
+    )
+
+    grad_hidden = run_combine(returned, hidden, grad, gain, ids)
+    scale = float(tokens * devices) ** (-0.5)
+    first, last, terms = project_hidden(grad_hidden, out_proj, gated, scale, ctx, exp)
+    terms = lax.all_to_all(terms, "exp", split_axis=0, concat_axis=0, tiled=True)
+
+    grads = run_backward(order, att, first, last, gain_heads, saved)
     grads = lax.all_to_all(grads, "ctx", split_axis=0, concat_axis=0, tiled=True)
 
-    scale = float(tokens * devices) ** (-0.5)
-    term = (scale * dot(hidden_all, gated.reshape(-1, 256), TN)).astype(BF16)
-    terms = lax.all_to_all(
-        term.reshape(exp, width // exp, 256), "exp", split_axis=0, concat_axis=0, tiled=True
-    )
-    grad_out_proj = vmem_call(sum_kernel, shape((width // exp, 256), F32), moved=MIB)(terms)
-
+    grad_out_proj = vmem_call(
+        sum_kernel, shape((width // exp, 256), F32), moved=MIB, limit=6, args=1
+    )(terms)
+
+    heads = decay_logit.shape[2]
     dq, dk, dv, dz, ddecay, dbeta = vmem_call(
         unpack_kernel,
         [
             shape(query_in.shape[1:]), shape(key_in.shape[1:]), shape(value_in.shape[1:]),
-            shape(gate_in.shape[1:]), shape(decay_logit.shape[1:]), shape(beta_logit.shape[1:]),
+            shape(gate_in.shape[1:]), shape((heads, tokens)), shape((heads, tokens)),
         ],
         moved=4 * MIB,
+        limit=12,
+        args=1,
     )(grads)
     return (
-        grad_hidden[None], dq[None], dk[None], dv[None], dz[None], ddecay[None], dbeta[None],
+        grad_hidden[None], dq[None], dk[None], dv[None], dz[None], ddecay.T[None], dbeta.T[None],
         grad_gate_up[None], grad_down[None], grad_out_proj,
     )
 

time: 285 us -> 223 us (0.78)
  Pallas kernels: 96.5 us -> 69.1 us
  blocking collectives: 19.3 us -> 0 us
  starting transfers between devices: 32.2 us -> 45.5 us
  between operations: 14.1 us -> 0.92 us
  local copies, waits for them, and re-layouts: 10.7 us -> 3.17 us
  matrix products: 13.3 us -> 8.73 us
  waiting for transfers between devices: 97.1 us -> 93.5 us
    all_to_all x1, waiting for transfers between devices: 20.7 us -> 49.2 us  [body(): lax.all_to_all(rows.reshape(devices, 8, width), ('ctx', 'exp'), split_axi...]
    pallas_call x6 -> x8, Pallas kernels: 72.1 us -> 45.9 us  [the longest x1 17.7 us: run_forward(): vmem_call(forward_kernel, [shape((blocks, 256, 128)), shape((blocks, 128,...]
    all_to_all x1, waiting for transfers between devices: 27.7 us -> 6.87 us  [body(): att = lax.all_to_all(packed, 'ctx', split_axis=0, concat_axis=0, tiled=True)]
    all_to_all x1 -> x0, blocking collectives: 19.3 us -> none  [body(): lax.all_to_all(dgated, 'ctx', split_axis=0, concat_axis=0, tiled=True)]
    all_to_all x1, waiting for transfers between devices: 20.3 us -> 2.37 us  [body(): lax.all_to_all(back.reshape(devices, 8, width // 2), ('ctx', 'exp'), spli...]
    ppermute x0 -> x9, waiting for transfers between devices: none -> 14.1 us  [the longest x4 14.1 us: send(): return lax.ppermute(x, 'ctx', [(i, (i + step) % ctx) for i in range(ctx)])]
    ppermute x0 -> x9, starting transfers between devices: none -> 13.2 us  [the longest x5 9.36 us: swap(): return lax.ppermute(x, 'ctx', [(i, i ^ 1) for i in range(ctx)])]
    all_to_all x1, waiting for transfers between devices: 10.5 us -> 0.01 us  [body(): lax.all_to_all(terms, 'exp', split_axis=0, concat_axis=0, tiled=True)]
  transfers between devices with their start and end apart: 7 -> 14, of which waited for: 5 -> 7; matrix products, arithmetic and copies ran while one was open for 7% -> 4% of each run, Pallas kernels for 30% -> 26%
where the time goes in v2:
time: 223 us; the launch traced here: 222 us
  waiting for transfers between devices  93.5 us (42%)
  Pallas kernels  69.1 us (31%)
  starting transfers between devices  45.5 us (20%)
  matrix products  8.73 us (4%)
  local copies, waits for them, and re-layouts  3.17 us (1%)
    all_to_all x1, waiting for transfers between devices, body(): lax.all_to_all(rows.reshape(devices, 8, width), ('ctx', 'exp'), split_axi...  49.2 us
    pallas_call x1, Pallas kernels, run_backward(): vmem_call(backward_kernel, shape((blocks, 136, 768)), [pltpu.VMEM((blocks...  21.9 us
    all_to_all x1, waiting for transfers between devices, body(): lax.all_to_all(grads, 'ctx', split_axis=0, concat_axis=0, tiled=True)  20.9 us
    pallas_call x1, Pallas kernels, run_forward(): vmem_call(forward_kernel, [shape((blocks, 256, 128)), shape((blocks, 128,...  17.7 us
    pallas_call x1, Pallas kernels, run_experts(): pl.pallas_call(expert_kernel, in_specs=[pl.BlockSpec(memory_space=pltpu.V...  14.9 us
    ppermute x4, waiting for transfers between devices, send(): return lax.ppermute(x, 'ctx', [(i, (i + step) % ctx) for i in range(ctx)])  14.1 us
    all_to_all x1, starting transfers between devices, body(): lax.all_to_all(rows.reshape(devices, 8, width), ('ctx', 'exp'), split_axi...  12 us
    ppermute x5, starting transfers between devices, swap(): return lax.ppermute(x, 'ctx', [(i, i ^ 1) for i in range(ctx)])  9.36 us
  transfers between devices with their start and end apart: 14, of which 7 were waited for; matrix products, arithmetic and copies ran while one was open for 4% of the time, Pallas kernels for 26%

profile of v2, /device:TPU:1, one launch (start us, length us, event | category | flops | bytes accessed | tf_op | source)
XLA Modules:
  0.0 221.9 jit_solution(12388491280401872086)
XLA Ops:
  0.6 5.5 %shard_map.240 = bf16[1024,2048]{1,0:T(8,128)(2,1)} custom-call(bf16[128,2048]{1,0:T(8,128)(2,1)} %bitcast.42, bf16[128,2048]{1,0:T(8,128)(2,1)} %bitcast.44, f32[1,2048]{1,0:T(1,128)} %bitcast.48, s32[10,1,128]{2,1,0:T(1,128)} %bitcast.50, f32[10,1,128]{2,1,0:T(1,128)} %bitcast.57), custom_call_target="tpu_custom_call" | custom-call | flops 1000000000 | bytes 6291456 | tf_op jit(solution)/shard_map/pallas_call | solution.py:659
  6.2 12.0 %all-to-all-start = ((bf16[128,8,2048]{2,1,0:T(8,128)(2,1)}), bf16[128,8,2048]{2,1,0:T(8,128)(2,1)}, u32[]{:S(2)}, u32[]{:S(2)}) async-start(bf16[128,8,2048]{2,1,0:T(8,128)(2,1)} %bitcast.55), calls=%async_computation | async-start | bytes 8388608 | tf_op jit(solution)/shard_map/all_to_all | solution.py:775
  18.2 1.4 shard_map.241
  19.6 49.2 %all-to-all-done = bf16[128,8,2048]{2,1,0:T(8,128)(2,1)} async-done(((bf16[128,8,2048]{2,1,0:T(8,128)(2,1)}), bf16[128,8,2048]{2,1,0:T(8,128)(2,1)}, u32[]{:S(2)}, u32[]{:S(2)}) %all-to-all-start) | async-done | bytes 4194336 | tf_op jit(solution)/shard_map/all_to_all | solution.py:775
  68.9 5.9 %all-to-all-start.1 = ((bf16[8,136,768]{2,1,0:T(8,128)(2,1)}), bf16[8,136,768]{2,1,0:T(8,128)(2,1)S(1)}, u32[]{:S(2)}, u32[]{:S(2)}) async-start(bf16[8,136,768]{2,1,0:T(8,128)(2,1)} %shard_map.241), calls=%async_computation.1 | async-start | bytes 3342336 | tf_op jit(solution)/shard_map/all_to_all | solution.py:783
  74.7 14.9 %shard_map.242 = (bf16[1024,1024]{1,0:T(8,128)(2,1)}, bf16[512,2048]{1,0:T(8,128)(2,1)}, bf16[512,2048]{1,0:T(8,128)(2,1)}, bf16[512,512]{1,0:T(8,128)(2,1)}, bf16[512,1024]{1,0:T(8,128)(2,1)}) custom-call(bf16[1024,2048]{1,0:T(8,128)(2,1)} %bitcast.6.got_ref, bf16[2048,1024]{1,0:T(8,128)(2,1)} %bitcast.58, bf16[512,2048]{1,0:T(8,128)(2,1)} %bitcast.59), custom_call_target="tpu_custom_call" | custom-call | flops 6000000000 | bytes 18874368 | tf_op jit(solution)/shard_map/pallas_call | solution.py:682
  89.6 6.9 %all-to-all-done.1.att_ref = bf16[8,136,768]{2,1,0:T(8,128)(2,1)S(1)} async-done(((bf16[8,136,768]{2,1,0:T(8,128)(2,1)}), bf16[8,136,768]{2,1,0:T(8,128)(2,1)S(1)}, u32[]{:S(2)}, u32[]{:S(2)}) %all-to-all-start.1) | async-done | bytes 1671200 | tf_op jit(solution)/shard_map/all_to_all | solution.py:783
  96.5 1.2 copy-done.15
  97.7 4.3 %all-to-all-start.2 = ((bf16[128,8,1024]{2,1,0:T(8,128)(2,1)}), bf16[128,8,1024]{2,1,0:T(8,128)(2,1)S(1)}, u32[]{:S(2)}, u32[]{:S(2)}) async-start(bf16[128,8,1024]{2,1,0:T(8,128)(2,1)} %bitcast.56), calls=%async_computation.2 | async-start | bytes 4194304 | tf_op jit(solution)/shard_map/all_to_all | solution.py:787
  102.6 4.3 %convolution_convert_fusion.1 = bf16[512,2048]{1,0:T(8,128)(2,1)} fusion(bf16[512,512]{1,0:T(8,128)(2,1)S(1)} %copy-done.18, bf16[512,2048]{1,0:T(8,128)(2,1)} %get-tuple-element.64), kind=kOutput, calls=%fused_computation.1 | convolution fusion | flops 1074790400 | bytes 4718592 | tf_op jit(solution)/shard_map/dot_general | solution.py:22
  106.9 4.4 %convolution_convert_fusion = bf16[2048,1024]{1,0:T(8,128)(2,1)} fusion(bf16[512,2048]{1,0:T(8,128)(2,1)S(1)} %copy-done.19, bf16[512,1024]{1,0:T(8,128)(2,1)S(1)} %copy-done.20), kind=kOutput, calls=%fused_computation | convolution fusion | flops 2149580800 | bytes 7340032 | tf_op jit(solution)/shard_map/dot_general | solution.py:22
  111.3 17.7 %shard_map.243 = (bf16[8,256,128]{2,1,0:T(8,128)(2,1)}, bf16[8,128,512]{2,1,0:T(8,128)(2,1)}, bf16[8,128,256]{2,1,0:T(8,128)(2,1)}, bf16[8,128,256]{2,1,0:T(8,12...) custom-call(s32[8]{0:T(128)} %compare_select_fusion.6.slot_ref, ...), custom_call_target="tpu_custom_call" | custom-call | flops 4000000000 | bytes 8388608 | tf_op jit(solution)/shard_map/pallas_call | solution.py:618
  129.0 2.4 %all-to-all-done.2 = bf16[128,8,1024]{2,1,0:T(8,128)(2,1)S(1)} async-done(((bf16[128,8,1024]{2,1,0:T(8,128)(2,1)}), bf16[128,8,1024]{2,1,0:T(8,128)(2,1)S(1)}, u32[]{:S(2)}, u32[]{:S(2)}) %all-to-all-start.2) | async-done | bytes 2097184 | tf_op jit(solution)/shard_map/all_to_all | solution.py:787
  131.4 2.1 shard_map.244.a_ref
  133.5 1.2 collective-permute-start.2
  135.0 2.1 collective-permute-start
  137.1 8.6 %collective-permute-done.2.d_ref = bf16[128,2048]{1,0:T(8,128)(2,1)S(1)} collective-permute-done((bf16[128,2048]{1,0:T(8,128)(2,1)}, bf16[128,2048]{1,0:T(8,128)(2,1)S(1)}, u32[]{:S(2)}, u32[]{:S(2)}) %collective-permute-start.2) | collective-permute-done | bytes 524320 | tf_op jit(solution)/shard_map/ppermute | solution.py:726
  145.7 2.3 %collective-permute-start.6 = (bf16[64,2048]{1,0:T(8,128)(2,1)S(1)}, bf16[64,2048]{1,0:T(8,128)(2,1)S(1)}, u32[]{:S(2)}, u32[]{:S(2)}) collective-permute-start(bf16[64,2048]{1,0:T(8,128)(2,1)S(1)} %slice.9), channel_id=1, source_target_pairs={{0,96},{16,112},{32,0},{48,16},{64,32},{80,48},{96,64},{112,80},{1... | collective-permute-start | bytes 786440 | tf_op jit(solution)/shard_map/ppermute | solution.py:726
  148.0 2.9 %collective-permute-start.4 = (bf16[128,2048]{1,0:T(8,128)(2,1)S(1)}, bf16[128,2048]{1,0:T(8,128)(2,1)S(1)}, u32[]{:S(2)}, u32[]{:S(2)}) collective-permute-start(bf16[128,2048]{1,0:T(8,128)(2,1)S(1)} %collective-permute-done.2.d_ref), channel_id=1, source_target_pairs={{0,16},{16,0},{32,48},{48,32},{64,80},{80,64},{96,112},{112,96},{1... | collective-permute-start | bytes 1572872 | tf_op jit(solution)/shard_map/ppermute | solution.py:729
  151.3 3.5 %collective-permute-start.8 = (bf16[64,2048]{1,0:T(8,128)(2,1)S(1)}, bf16[64,2048]{1,0:T(8,128)(2,1)S(1)}, u32[]{:S(2)}, u32[]{:S(2)}) collective-permute-start(bf16[64,2048]{1,0:T(8,128)(2,1)S(1)} %collective-permute-done.6.c1_ref), channel_id=1, source_target_pairs={{0,16},{16,0},{32,48},{48,32},{64,80},{80,64},{96,112},{112,96},{1... | collective-permute-start | bytes 786440 | tf_op jit(solution)/shard_map/ppermute | solution.py:729
  154.8 5.4 %collective-permute-done.5.c0_ref = bf16[64,2048]{1,0:T(8,128)(2,1)S(1)} collective-permute-done((bf16[64,2048]{1,0:T(8,128)(2,1)S(1)}, bf16[64,2048]{1,0:T(8,128)(2,1)S(1)}, u32[]{:S(2)}, u32[]{:S(2)}) %collective-permute-start.5) | collective-permute-done | bytes 262176 | tf_op jit(solution)/shard_map/ppermute | solution.py:726
  160.1 0.8 collective-permute-start.7
  160.9 1.0 copy-done.12
  162.0 1.2 shard_map.245
  163.3 2.2 %shard_map.246 = (f32[4,128,256]{2,1,0:T(8,128)S(1)}, bf16[16,256,128]{2,1,0:T(8,128)(2,1)}) custom-call(bf16[128,2048]{1,0:T(8,128)(2,1)S(1)} %collective-permute-done.3.a_ref, bf16[128,2048]{1,0:T(8,128)(2,1)S(1)} %collective-permute-done.4.b_ref, bf16[64,2048]{1,0:T(8,128)(2,1)S(1)} %collective-permute-done.5.c0_ref, ...), custom_call_target="tpu_custom_call" | custom-call | flops 1000000000 | bytes 7340032 | tf_op jit(solution)/shard_map/pallas_call | solution.py:745
  165.5 0.8 copy-done.13
  166.3 6.4 %all-to-all-start.4 = ((bf16[16,256,128]{2,1,0:T(8,128)(2,1)}), bf16[16,256,128]{2,1,0:T(8,128)(2,1)S(1)}, u32[]{:S(2)}, u32[]{:S(2)}) async-start(bf16[16,256,128]{2,1,0:T(8,128)(2,1)} %get-tuple-element.85), calls=%async_computation.4 | async-start | bytes 2097152 | tf_op jit(solution)/shard_map/all_to_all | solution.py:800
  173.2 21.9 %shard_map.247 = bf16[8,136,768]{2,1,0:T(8,128)(2,1)} custom-call(s32[8]{0:T(128)} %fusion.1.order_ref, bf16[8,136,768]{2,1,0:T(8,128)(2,1)} %copy-done.15, f32[4,128,256]{2,1,0:T(8,128)} %copy-done.14, f32[4,128,256]{2,1,0:T(8,128)} %copy-done.13, f32[1,128]{1,0:T(1,128)} %bitcast.67, bf16[8,128,512]{2,1,0:T(8,128)(2,1)} %get-tuple-element.70.tinv_ref, ...), custom_call_target="tpu_custom_call" | custom-call | flops 6000000000 | bytes 8388608 | tf_op jit(solution)/shard_map/pallas_call | solution.py:638
  195.2 3.8 %all-to-all-start.3 = ((bf16[8,136,768]{2,1,0:T(8,128)(2,1)}), bf16[8,136,768]{2,1,0:T(8,128)(2,1)S(1)}, u32[]{:S(2)}, u32[]{:S(2)}) async-start(bf16[8,136,768]{2,1,0:T(8,128)(2,1)} %shard_map.247), calls=%async_computation.3 | async-start | bytes 3342336 | tf_op jit(solution)/shard_map/all_to_all | solution.py:803
  198.9 0.9 shard_map.249
  199.8 20.9 %all-to-all-done.3.in_ref = bf16[8,136,768]{2,1,0:T(8,128)(2,1)S(1)} async-done(((bf16[8,136,768]{2,1,0:T(8,128)(2,1)}), bf16[8,136,768]{2,1,0:T(8,128)(2,1)S(1)}, u32[]{:S(2)}, u32[]{:S(2)}) %all-to-all-start.3) | async-done | bytes 1671200 | tf_op jit(solution)/shard_map/all_to_all | solution.py:803
  220.7 1.2 shard_map.248
  (54 shorter events, 1.8 us)
Async XLA Ops:
  6.2 12.0 %copy-start.1 = (bf16[1,128,2048]{2,1,0:T(8,128)(2,1)S(1)}, bf16[1,128,2048]{2,1,0:T(8,128)(2,1)}, u32[]{:S(2)}) copy-start(bf16[1,128,2048]{2,1,0:T(8,128)(2,1)} %param.26) | copy-start | bytes 1572868
  6.2 12.0 %copy-start.2 = (bf16[1,128,2048]{2,1,0:T(8,128)(2,1)S(1)}, bf16[1,128,2048]{2,1,0:T(8,128)(2,1)}, u32[]{:S(2)}) copy-start(bf16[1,128,2048]{2,1,0:T(8,128)(2,1)} %param.27) | copy-start | bytes 1572868
  6.2 12.0 %copy-start.6 = (bf16[1,128,1024]{2,1,0:T(8,128)(2,1)S(1)}, bf16[1,128,1024]{2,1,0:T(8,128)(2,1)}, u32[]{:S(2)}) copy-start(bf16[1,128,1024]{2,1,0:T(8,128)(2,1)} %param.24) | copy-start | bytes 786436
  6.2 12.0 %copy-start.7 = (bf16[1,128,1024]{2,1,0:T(8,128)(2,1)S(1)}, bf16[1,128,1024]{2,1,0:T(8,128)(2,1)}, u32[]{:S(2)}) copy-start(bf16[1,128,1024]{2,1,0:T(8,128)(2,1)} %param.25) | copy-start | bytes 786436
  6.2 12.0 %copy-start.10 = (bf16[1,128,16]{1,2,0:T(8,128)(2,1)S(1)}, bf16[1,128,16]{1,2,0:T(8,128)(2,1)}, u32[]{:S(2)}) copy-start(bf16[1,128,16]{1,2,0:T(8,128)(2,1)} %param.28) | copy-start | bytes 12292
  6.2 12.0 %copy-start.11 = (bf16[1,128,16]{1,2,0:T(8,128)(2,1)S(1)}, bf16[1,128,16]{1,2,0:T(8,128)(2,1)}, u32[]{:S(2)}) copy-start(bf16[1,128,16]{1,2,0:T(8,128)(2,1)} %param.29) | copy-start | bytes 12292
  6.2 62.6 %all-to-all-start = ((bf16[128,8,2048]{2,1,0:T(8,128)(2,1)}), bf16[128,8,2048]{2,1,0:T(8,128)(2,1)}, u32[]{:S(2)}, u32[]{:S(2)}) async-start(bf16[128,8,2048]{2,1,0:T(8,128)(2,1)} %bitcast.55), calls=%async_computation | async-start | bytes 8388608 | tf_op jit(solution)/shard_map/all_to_all | solution.py:775
  68.9 27.6 %all-to-all-start.1 = ((bf16[8,136,768]{2,1,0:T(8,128)(2,1)}), bf16[8,136,768]{2,1,0:T(8,128)(2,1)S(1)}, u32[]{:S(2)}, u32[]{:S(2)}) async-start(bf16[8,136,768]{2,1,0:T(8,128)(2,1)} %shard_map.241), calls=%async_computation.1 | async-start | bytes 3342336 | tf_op jit(solution)/shard_map/all_to_all | solution.py:783
  96.5 6.1 %copy-start.18 = (bf16[512,512]{1,0:T(8,128)(2,1)S(1)}, bf16[512,512]{1,0:T(8,128)(2,1)}, u32[]{:S(2)}) copy-start(bf16[512,512]{1,0:T(8,128)(2,1)} %get-tuple-element.63) | copy-start | bytes 1572868
  97.7 33.7 %all-to-all-start.2 = ((bf16[128,8,1024]{2,1,0:T(8,128)(2,1)}), bf16[128,8,1024]{2,1,0:T(8,128)(2,1)S(1)}, u32[]{:S(2)}, u32[]{:S(2)}) async-start(bf16[128,8,1024]{2,1,0:T(8,128)(2,1)} %bitcast.56), calls=%async_computation.2 | async-start | bytes 4194304 | tf_op jit(solution)/shard_map/all_to_all | solution.py:787
  102.6 4.3 %copy-start.19 = (bf16[512,2048]{1,0:T(8,128)(2,1)S(1)}, bf16[512,2048]{1,0:T(8,128)(2,1)}, u32[]{:S(2)}) copy-start(bf16[512,2048]{1,0:T(8,128)(2,1)} %get-tuple-element.61) | copy-start | bytes 6291460
  102.6 4.3 %copy-start.20 = (bf16[512,1024]{1,0:T(8,128)(2,1)S(1)}, bf16[512,1024]{1,0:T(8,128)(2,1)}, u32[]{:S(2)}) copy-start(bf16[512,1024]{1,0:T(8,128)(2,1)} %get-tuple-element.62) | copy-start | bytes 3145732
  111.3 20.1 %copy-start.3 = (bf16[1,128,2048]{2,1,0:T(8,128)(2,1)S(1)}, bf16[1,128,2048]{2,1,0:T(8,128)(2,1)}, u32[]{:S(2)}) copy-start(bf16[1,128,2048]{2,1,0:T(8,128)(2,1)} %param.17) | copy-start | bytes 1572868
  111.3 20.1 %copy-start.4 = (bf16[1,128,2048]{2,1,0:T(8,128)(2,1)S(1)}, bf16[1,128,2048]{2,1,0:T(8,128)(2,1)}, u32[]{:S(2)}) copy-start(bf16[1,128,2048]{2,1,0:T(8,128)(2,1)} %param.18) | copy-start | bytes 1572868
  111.3 20.1 %copy-start.8 = (f32[2048]{0:T(1024)S(1)}, f32[2048]{0:T(1024)}, u32[]{:S(2)}) copy-start(f32[2048]{0:T(1024)} %param.19) | copy-start | bytes 24580
  111.3 20.1 %copy-start.9 = (s32[1,128,10]{1,0,2:T(1,128)S(1)}, s32[1,128,10]{1,0,2:T(1,128)}, u32[]{:S(2)}) copy-start(s32[1,128,10]{1,0,2:T(1,128)} %param.20) | copy-start | bytes 15364
  131.4 29.5 %copy-start = (bf16[2048,256]{1,0:T(8,128)(2,1)S(1)}, bf16[2048,256]{1,0:T(8,128)(2,1)}, u32[]{:S(2)}) copy-start(bf16[2048,256]{1,0:T(8,128)(2,1)} %proj_ref.3) | copy-start | bytes 3145732
  131.4 29.5 %copy-start.5 = (bf16[8,256,128]{2,1,0:T(8,128)(2,1)S(1)}, bf16[8,256,128]{2,1,0:T(8,128)(2,1)}, u32[]{:S(2)}) copy-start(bf16[8,256,128]{2,1,0:T(8,128)(2,1)} %get-tuple-element.66.gated_ref) | copy-start | bytes 1572868
  133.5 12.1 %collective-permute-start.2 = (bf16[128,2048]{1,0:T(8,128)(2,1)}, bf16[128,2048]{1,0:T(8,128)(2,1)S(1)}, u32[]{:S(2)}, u32[]{:S(2)}) collective-permute-start(bf16[128,2048]{1,0:T(8,128)(2,1)} %shard_map.244.a_ref), channel_id=1, source_target_pairs={{0,96},{16,112},{32,0},{48,16},{64,32},{80,48},{96,64},{112,80},{1... | collective-permute-start | bytes 1572872 | tf_op jit(solution)/shard_map/ppermute | solution.py:726
  134.7 16.1 %collective-permute-start.1 = (bf16[128,2048]{1,0:T(8,128)(2,1)}, bf16[128,2048]{1,0:T(8,128)(2,1)S(1)}, u32[]{:S(2)}, u32[]{:S(2)}) collective-permute-start(bf16[128,2048]{1,0:T(8,128)(2,1)} %shard_map.244.a_ref), channel_id=1, source_target_pairs={{0,32},{16,48},{32,64},{48,80},{64,96},{80,112},{96,0},{112,16},{1... | collective-permute-start | bytes 1572872 | tf_op jit(solution)/shard_map/ppermute | solution.py:726
  135.0 25.9 %collective-permute-start = (bf16[128,2048]{1,0:T(8,128)(2,1)}, bf16[128,2048]{1,0:T(8,128)(2,1)S(1)}, u32[]{:S(2)}, u32[]{:S(2)}) collective-permute-start(bf16[128,2048]{1,0:T(8,128)(2,1)} %shard_map.244.a_ref), channel_id=1, source_target_pairs={{0,16},{16,0},{32,48},{48,32},{64,80},{80,64},{96,112},{112,96},{1... | collective-permute-start | bytes 1572872 | tf_op jit(solution)/shard_map/ppermute | solution.py:729
  145.7 5.6 %collective-permute-start.6 = (bf16[64,2048]{1,0:T(8,128)(2,1)S(1)}, bf16[64,2048]{1,0:T(8,128)(2,1)S(1)}, u32[]{:S(2)}, u32[]{:S(2)}) collective-permute-start(bf16[64,2048]{1,0:T(8,128)(2,1)S(1)} %slice.9), channel_id=1, source_target_pairs={{0,96},{16,112},{32,0},{48,16},{64,32},{80,48},{96,64},{112,80},{1... | collective-permute-start | bytes 786440 | tf_op jit(solution)/shard_map/ppermute | solution.py:726
  148.0 15.3 %collective-permute-start.4 = (bf16[128,2048]{1,0:T(8,128)(2,1)S(1)}, bf16[128,2048]{1,0:T(8,128)(2,1)S(1)}, u32[]{:S(2)}, u32[]{:S(2)}) collective-permute-start(bf16[128,2048]{1,0:T(8,128)(2,1)S(1)} %collective-permute-done.2.d_ref), channel_id=1, source_target_pairs={{0,16},{16,0},{32,48},{48,32},{64,80},{80,64},{96,112},{112,96},{1... | collective-permute-start | bytes 1572872 | tf_op jit(solution)/shard_map/ppermute | solution.py:729
  150.9 9.2 %collective-permute-start.5 = (bf16[64,2048]{1,0:T(8,128)(2,1)S(1)}, bf16[64,2048]{1,0:T(8,128)(2,1)S(1)}, u32[]{:S(2)}, u32[]{:S(2)}) collective-permute-start(bf16[64,2048]{1,0:T(8,128)(2,1)S(1)} %slice.8), channel_id=1, source_target_pairs={{0,32},{16,48},{32,64},{48,80},{64,96},{80,112},{96,0},{112,16},{1... | collective-permute-start | bytes 786440 | tf_op jit(solution)/shard_map/ppermute | solution.py:726
  151.0 12.3 %collective-permute-start.3 = (bf16[128,2048]{1,0:T(8,128)(2,1)S(1)}, bf16[128,2048]{1,0:T(8,128)(2,1)S(1)}, u32[]{:S(2)}, u32[]{:S(2)}) collective-permute-start(bf16[128,2048]{1,0:T(8,128)(2,1)S(1)} %collective-permute-done.1.c_ref), channel_id=1, source_target_pairs={{0,16},{16,0},{32,48},{48,32},{64,80},{80,64},{96,112},{112,96},{1... | collective-permute-start | bytes 1572872 | tf_op jit(solution)/shard_map/ppermute | solution.py:729
  151.3 11.9 %collective-permute-start.8 = (bf16[64,2048]{1,0:T(8,128)(2,1)S(1)}, bf16[64,2048]{1,0:T(8,128)(2,1)S(1)}, u32[]{:S(2)}, u32[]{:S(2)}) collective-permute-start(bf16[64,2048]{1,0:T(8,128)(2,1)S(1)} %collective-permute-done.6.c1_ref), channel_id=1, source_target_pairs={{0,16},{16,0},{32,48},{48,32},{64,80},{80,64},{96,112},{112,96},{1... | collective-permute-start | bytes 786440 | tf_op jit(solution)/shard_map/ppermute | solution.py:729
  160.1 3.1 %collective-permute-start.7 = (bf16[64,2048]{1,0:T(8,128)(2,1)S(1)}, bf16[64,2048]{1,0:T(8,128)(2,1)S(1)}, u32[]{:S(2)}, u32[]{:S(2)}) collective-permute-start(bf16[64,2048]{1,0:T(8,128)(2,1)S(1)} %collective-permute-done.5.c0_ref), channel_id=1, source_target_pairs={{0,16},{16,0},{32,48},{48,32},{64,80},{80,64},{96,112},{112,96},{1... | collective-permute-start | bytes 786440 | tf_op jit(solution)/shard_map/ppermute | solution.py:729
  163.2 2.3 %copy-start.14 = (f32[4,128,256]{2,1,0:T(8,128)}, f32[4,128,256]{2,1,0:T(8,128)S(1)}, u32[]{:S(2)}) copy-start(f32[4,128,256]{2,1,0:T(8,128)S(1)} %get-tuple-element.67.first_ref) | copy-start | bytes 1572868
  166.3 6.4 %copy-start.16 = (s32[8]{0:T(128)S(1)}, s32[8]{0:T(128)}, u32[]{:S(2)}) copy-start(s32[8]{0:T(128)} %constant.69.clone) | copy-start | bytes 100
  166.3 6.4 %copy-start.17 = (s32[8]{0:T(128)S(1)}, s32[8]{0:T(128)}, u32[]{:S(2)}) copy-start(s32[8]{0:T(128)} %constant.68.clone) | copy-start | bytes 100
  166.3 28.8 %all-to-all-start.4 = ((bf16[16,256,128]{2,1,0:T(8,128)(2,1)}), bf16[16,256,128]{2,1,0:T(8,128)(2,1)S(1)}, u32[]{:S(2)}, u32[]{:S(2)}) async-start(bf16[16,256,128]{2,1,0:T(8,128)(2,1)} %get-tuple-element.85), calls=%async_computation.4 | async-start | bytes 2097152 | tf_op jit(solution)/shard_map/all_to_all | solution.py:800
  195.2 25.6 %all-to-all-start.3 = ((bf16[8,136,768]{2,1,0:T(8,128)(2,1)}), bf16[8,136,768]{2,1,0:T(8,128)(2,1)S(1)}, u32[]{:S(2)}, u32[]{:S(2)}) async-start(bf16[8,136,768]{2,1,0:T(8,128)(2,1)} %shard_map.247), calls=%async_computation.3 | async-start | bytes 3342336 | tf_op jit(solution)/shard_map/all_to_all | solution.py:803
  (3 other events, 3.1 us)
